TPU v7x, 128 devices: a whole 4x4x4 slice. The times are simulated.
128 devices in a mesh: ctx: 32 (over y, z, core), head: 4 (over x).
Axes of the slice: x: 4, y: 4, z: 4, core: 2. Of those that a mesh axis runs over, the one named last changes fastest.
Arguments:
- entries: bfloat16 [65536, 2048], P('ctx', 'head'), may hold values from -6 to 6
- gating: bfloat16 [65536, 2048], P('ctx', 'head'), may hold values from -6 to 6
- state_in: bfloat16 [65536, 128], P('ctx'), may hold values from -2 to 2
- state_out: bfloat16 [65536, 128], P('ctx'), may hold values from -2 to 2
- step_size: float32 [32, 65536], P('head', 'ctx'), may hold values from 0.2 to 1.5
- decay_rate: float32 [32], P('head'), may hold values from 1.5258789e-06 to 0.1
- skip_gain: float32 [32], P('head'), may hold values from 0.5 to 1.5
- level_gate: float32 [32, 5, 65536], P('head', None, 'ctx'), may hold values from 0.2 to 1.5
- norm_gain: float32 [2048], P('head'), may hold values from 0.5 to 1.5
- cotangent: bfloat16 [65536, 2048], P('ctx'), may hold values from -0.119628906 to 0.119628906
- master_weight: float32 [2048, 2048], P('ctx', 'head'), may hold values from -0.125 to 0.125
- first_moment: float32 [2048, 2048], P('ctx', 'head'), may hold values from -3 to 3
- second_moment: float32 [2048, 2048], P('ctx', 'head'), may hold values from 0.1 to 10
Outputs:
- normed: bfloat16 [65536, 2048], P('ctx', 'head')
- weights: bfloat16 [2048, 2048], P(None, 'head')
- gradient: float32 [2048, 2048], P('ctx', 'head')
All inputs are finite; a program needn't handle non-finite values.
Results may differ from a plain program's by a relative error of at most 0.0059.
Values may be sent and summed in bfloat16 or wider, within the bound.
A program may use at most 128 MiB of HBM per device.

v0:
```python
import jax
import jax.numpy as jnp
from jax import lax
from jax.sharding import PartitionSpec as P

HEAD_DIM = 64
BLOCK = 256
INNER = 2048


def block_scan(scaled, state_in, state_out, log_decay):
    length, head_count, head_width = scaled.shape
    state_width = state_in.shape[1]
    blocks = length // BLOCK
    decay_blocks = log_decay.reshape(head_count, blocks, BLOCK).transpose(1, 0, 2)
    value_blocks = scaled.reshape(blocks, BLOCK, head_count, head_width)
    in_blocks = state_in.reshape(blocks, BLOCK, state_width)
    out_blocks = state_out.reshape(blocks, BLOCK, state_width)
    causal = jnp.arange(BLOCK)[:, None] >= jnp.arange(BLOCK)[None, :]

    def advance(running, pieces):
        decays, value_block, in_block, out_block = pieces
        prefix = jnp.cumsum(decays, axis=-1)
        scores = jnp.dot(out_block, in_block.T, preferred_element_type=jnp.float32)
        gap_matrix = jnp.where(causal[None], prefix[:, :, None] - prefix[:, None, :], 0.0)
        decay_mask = jnp.where(causal[None], jnp.exp(gap_matrix), 0.0)
        mix = (scores[None] * decay_mask).astype(jnp.bfloat16)
        within = jnp.einsum("hts,shp->thp", mix, value_block, preferred_element_type=jnp.float32)
        carried = jnp.einsum(
            "tn,hpn->thp",
            out_block,
            running.astype(jnp.bfloat16),
            preferred_element_type=jnp.float32,
        )
        carried = carried * jnp.exp(prefix).T[:, :, None]
        to_end = (
            value_block.astype(jnp.float32) * jnp.exp(prefix[:, -1:] - prefix).T[:, :, None]
        ).astype(jnp.bfloat16)
        update = jnp.einsum("thp,tn->hpn", to_end, in_block, preferred_element_type=jnp.float32)
        running = jnp.exp(prefix[:, -1])[:, None, None] * running + update
        return (running, (within + carried, prefix))

    start = jnp.zeros((head_count, head_width, state_width), jnp.float32)
    end_state, (outputs, prefixes) = lax.scan(
        advance, start, (decay_blocks, value_blocks, in_blocks, out_blocks)
    )
    totals = prefixes[:, :, -1]
    offsets = jnp.cumsum(totals, axis=0) - totals
    cumulative = (prefixes + offsets[:, :, None]).transpose(1, 0, 2).reshape(head_count, length)
    return (outputs.reshape(length, head_count, head_width), end_state, cumulative)


def level_states(all_ends, all_totals, position, depth):
    members = all_ends.shape[0]
    positions = jnp.arange(members, dtype=jnp.int32)
    between = (positions[None, :] > positions[:, None]) & (positions[None, :] < position)
    gap_decay = jnp.sum(jnp.where(between[:, :, None], all_totals[None, :, :], 0.0), axis=1)
    collected = []
    for rung in range(depth):
        selected = (positions < position) & (
            jnp.right_shift(positions, rung + 1) == jnp.right_shift(position, rung + 1)
        )
        selected = selected & (jnp.bitwise_and(jnp.right_shift(position, rung), 1) == 1)
        selected = selected & (jnp.bitwise_and(jnp.right_shift(positions, rung), 1) == 0)
        factor = jnp.where(selected[:, None], jnp.exp(gap_decay), 0.0)
        collected.append(
            jnp.einsum("jh,jhpn->hpn", factor, all_ends, precision=lax.Precision.HIGHEST)
        )
    return collected


def finish(within, cumulative, by_head, gating, state_out, gate_rows, skip_gain, levels):
    length, head_count, head_width = within.shape
    across = jnp.zeros_like(within)
    for rung, level_state in enumerate(levels):
        readout = jnp.einsum(
            "tn,hpn->thp",
            state_out,
            level_state.astype(jnp.bfloat16),
            preferred_element_type=jnp.float32,
        )
        across = across + readout * gate_rows[:, rung, :].T[:, :, None]
    mixed = (
        within
        + across * jnp.exp(cumulative).T[:, :, None]
        + skip_gain[None, :, None] * by_head.astype(jnp.float32)
    )
    return mixed.reshape(length, head_count * head_width) * jax.nn.silu(gating.astype(jnp.float32))


def adamw(gradient, master, moment_one, moment_two):
    moment_one = 0.9 * moment_one + 0.1 * gradient
    moment_two = 0.95 * moment_two + 0.05 * gradient * gradient
    ratio = moment_one / (1.0 - 0.9**10) / (jnp.sqrt(moment_two / (1.0 - 0.95**10)) + 1e-08)
    return (master - 0.1 * (ratio + 0.1 * master)).astype(jnp.bfloat16)


def on_device(
    entries,
    gating,
    state_in,
    state_out,
    step_size,
    decay_rate,
    skip_gain,
    level_gate,
    norm_gain,
    cotangent,
    master_weight,
    first_moment,
    second_moment,
):
    length = entries.shape[0]
    head_count = decay_rate.shape[0]
    by_head = entries.reshape(length, head_count, HEAD_DIM)
    log_decay = -decay_rate[:, None] * step_size
    scaled = (by_head.astype(jnp.float32) * step_size.T[:, :, None]).astype(jnp.bfloat16)
    within, end_state, cumulative = block_scan(scaled, state_in, state_out, log_decay)
    decay_sum = cumulative[:, -1]
    position = lax.axis_index("ctx")
    depth = lax.axis_size("ctx").bit_length() - 1
    all_ends, all_totals = (
        lax.all_gather(end_state[None], "ctx", axis=0, tiled=True),
        lax.all_gather(decay_sum[None], "ctx", axis=0, tiled=True),
    )
    levels = level_states(all_ends, all_totals, position, depth)
    gated = finish(within, cumulative, by_head, gating, state_out, level_gate, skip_gain, levels)
    square_sums = lax.psum(jnp.sum(gated * gated, axis=1), "head")
    mean_sq = square_sums / INNER
    normed = (gated * lax.rsqrt(mean_sq + 1e-05)[:, None] * norm_gain[None, :]).astype(jnp.bfloat16)
    gradient = lax.psum_scatter(
        lax.dot_general(
            cotangent, normed, (((0,), (0,)), ((), ())), preferred_element_type=jnp.float32
        ),
        "ctx",
        scatter_dimension=0,
        tiled=True,
    )
    updated = adamw(gradient, master_weight, first_moment, second_moment)
    weights = lax.all_gather(updated, "ctx", axis=0, tiled=True)
    return (normed, weights, gradient)


def solution(mesh):
    return jax.shard_map(
        on_device,
        mesh=mesh,
        in_specs=(
            P("ctx", "head"),
            P("ctx", "head"),
            P("ctx", None),
            P("ctx", None),
            P("head", "ctx"),
            P("head"),
            P("head"),
            P("head", None, "ctx"),
            P("head"),
            P("ctx", None),
            P("ctx", "head"),
            P("ctx", "head"),
            P("ctx", "head"),
        ),
        out_specs=(P("ctx", "head"), P(None, "head"), P("ctx", "head")),
        check_vma=False,
    )
```

profile of v0, /device:TPU:1, one launch (start us, length us, event | category | flops | bytes accessed | tf_op | source)
XLA Modules:
  0.0 470.7 jit_solution(6927622259204467229)
XLA Ops:
  9.7 4.2 copy.84
  13.9 4.1 copy.114
  19.0 140.8 %while.16 = (s32[]{:T(128)}, f32[8,64,128]{2,1,0:T(8,128)S(1)}, f32[8,256,8,64]{1,0,3,2:T(8,128)}, f32[8,8,256]{2,1,0:T(8,128)S(1)}, f32[8,8,256]{2,1,0:T(8,128)...) while((s32[]{:T(128)}, f32[8,64,128]{2,1,0:T(8,128)S(1)}, ...), condition=%wide.region_3.4_spmd.clone.clone, body=%wide.region_0.3_spmd.clone.clone.sunk | while | flops 154865696 | bytes 6026011 | solution.py:44
  23.9 12.7 %dynamic_update_slice.16 = f32[8,256,8,64]{1,0,3,2:T(8,128)} dynamic-update-slice(f32[8,256,8,64]{1,0,3,2:T(8,128)} %get-tuple-element.265, f32[1,256,8,64]{1,0,3,2:T(1,128)S(1)} %copy.126, s32[]{:T(128)S(6)} %copy.133, s32[]{:T(128)} %constant.27.clone.1..sunk, s32[]{:T(128)} %constant.27.clone.1..sunk, s32[]{:T(128)} %constant.27.clone.1..sunk) | dynamic-update-slice | bytes 1048580 | tf_op jit(solution)/shard_map/while/body/jit(dynamic_update_index_in_dim)/dynamic_update_slice | solution.py:44
  41.5 12.7 %dynamic_update_slice.16 = f32[8,256,8,64]{1,0,3,2:T(8,128)} dynamic-update-slice(f32[8,256,8,64]{1,0,3,2:T(8,128)} %get-tuple-element.265, f32[1,256,8,64]{1,0,3,2:T(1,128)S(1)} %copy.126, s32[]{:T(128)S(6)} %copy.133, s32[]{:T(128)} %constant.27.clone.1..sunk, s32[]{:T(128)} %constant.27.clone.1..sunk, s32[]{:T(128)} %constant.27.clone.1..sunk) | dynamic-update-slice | bytes 1048580 | tf_op jit(solution)/shard_map/while/body/jit(dynamic_update_index_in_dim)/dynamic_update_slice | solution.py:44
  59.1 12.7 %dynamic_update_slice.16 = f32[8,256,8,64]{1,0,3,2:T(8,128)} dynamic-update-slice(f32[8,256,8,64]{1,0,3,2:T(8,128)} %get-tuple-element.265, f32[1,256,8,64]{1,0,3,2:T(1,128)S(1)} %copy.126, s32[]{:T(128)S(6)} %copy.133, s32[]{:T(128)} %constant.27.clone.1..sunk, s32[]{:T(128)} %constant.27.clone.1..sunk, s32[]{:T(128)} %constant.27.clone.1..sunk) | dynamic-update-slice | bytes 1048580 | tf_op jit(solution)/shard_map/while/body/jit(dynamic_update_index_in_dim)/dynamic_update_slice | solution.py:44
  76.7 12.7 %dynamic_update_slice.16 = f32[8,256,8,64]{1,0,3,2:T(8,128)} dynamic-update-slice(f32[8,256,8,64]{1,0,3,2:T(8,128)} %get-tuple-element.265, f32[1,256,8,64]{1,0,3,2:T(1,128)S(1)} %copy.126, s32[]{:T(128)S(6)} %copy.133, s32[]{:T(128)} %constant.27.clone.1..sunk, s32[]{:T(128)} %constant.27.clone.1..sunk, s32[]{:T(128)} %constant.27.clone.1..sunk) | dynamic-update-slice | bytes 1048580 | tf_op jit(solution)/shard_map/while/body/jit(dynamic_update_index_in_dim)/dynamic_update_slice | solution.py:44
  94.3 12.7 %dynamic_update_slice.16 = f32[8,256,8,64]{1,0,3,2:T(8,128)} dynamic-update-slice(f32[8,256,8,64]{1,0,3,2:T(8,128)} %get-tuple-element.265, f32[1,256,8,64]{1,0,3,2:T(1,128)S(1)} %copy.126, s32[]{:T(128)S(6)} %copy.133, s32[]{:T(128)} %constant.27.clone.1..sunk, s32[]{:T(128)} %constant.27.clone.1..sunk, s32[]{:T(128)} %constant.27.clone.1..sunk) | dynamic-update-slice | bytes 1048580 | tf_op jit(solution)/shard_map/while/body/jit(dynamic_update_index_in_dim)/dynamic_update_slice | solution.py:44
  111.9 12.7 %dynamic_update_slice.16 = f32[8,256,8,64]{1,0,3,2:T(8,128)} dynamic-update-slice(f32[8,256,8,64]{1,0,3,2:T(8,128)} %get-tuple-element.265, f32[1,256,8,64]{1,0,3,2:T(1,128)S(1)} %copy.126, s32[]{:T(128)S(6)} %copy.133, s32[]{:T(128)} %constant.27.clone.1..sunk, s32[]{:T(128)} %constant.27.clone.1..sunk, s32[]{:T(128)} %constant.27.clone.1..sunk) | dynamic-update-slice | bytes 1048580 | tf_op jit(solution)/shard_map/while/body/jit(dynamic_update_index_in_dim)/dynamic_update_slice | solution.py:44
  129.5 12.7 %dynamic_update_slice.16 = f32[8,256,8,64]{1,0,3,2:T(8,128)} dynamic-update-slice(f32[8,256,8,64]{1,0,3,2:T(8,128)} %get-tuple-element.265, f32[1,256,8,64]{1,0,3,2:T(1,128)S(1)} %copy.126, s32[]{:T(128)S(6)} %copy.133, s32[]{:T(128)} %constant.27.clone.1..sunk, s32[]{:T(128)} %constant.27.clone.1..sunk, s32[]{:T(128)} %constant.27.clone.1..sunk) | dynamic-update-slice | bytes 1048580 | tf_op jit(solution)/shard_map/while/body/jit(dynamic_update_index_in_dim)/dynamic_update_slice | solution.py:44
  147.1 12.7 %dynamic_update_slice.16 = f32[8,256,8,64]{1,0,3,2:T(8,128)} dynamic-update-slice(f32[8,256,8,64]{1,0,3,2:T(8,128)} %get-tuple-element.265, f32[1,256,8,64]{1,0,3,2:T(1,128)S(1)} %copy.126, s32[]{:T(128)S(6)} %copy.133, s32[]{:T(128)} %constant.27.clone.1..sunk, s32[]{:T(128)} %constant.27.clone.1..sunk, s32[]{:T(128)} %constant.27.clone.1..sunk) | dynamic-update-slice | bytes 1048580 | tf_op jit(solution)/shard_map/while/body/jit(dynamic_update_index_in_dim)/dynamic_update_slice | solution.py:44
  162.9 66.0 %all-reduce = f32[256]{0:T(256)S(1)} all-reduce(f32[256]{0:T(256)S(1)} %dynamic-update-slice), channel_id=2, replica_groups=mesh['ctx'=32,'head'=4] {'ctx'}, use_global_device_ids=true, to_apply=%add | all-reduce | flops 256 | bytes 2048
  229.6 5.0 %reshape.209 = f32[2048,8,64]{0,2,1:T(8,128)} reshape(f32[8,256,8,64]{1,0,3,2:T(8,128)} %get-tuple-element.55) | data formatting | bytes 8388608 | tf_op jit(solution)/shard_map/reshape | solution.py:50
  234.7 12.7 %fusion.40 = f32[8,1,64,128]{3,1,2,0:T(1,128)S(1)} fusion(f32[32,8,1,1]{0,2,3,1:T(1,128)S(1)} %copy.96, f32[32,8,64,128]{3,2,1,0:T(8,128)} %bitcast.182), kind=kOutput, calls=%fused_computation.52 | convolution fusion | flops 25165824 | bytes 8651776 | tf_op jit(solution)/shard_map/jh,jhpn->hpn/dot_general | solution.py:67
  247.5 8.6 %fusion.34 = f32[8,1,64,128]{3,1,2,0:T(1,128)S(1)} fusion(f32[32,8,1,1]{0,2,3,1:T(1,128)S(1)} %copy.103, f32[32,8,64,128]{3,2,1,0:T(8,128)S(1)} %bitcast.183), kind=kOutput, calls=%fused_computation.46 | convolution fusion | flops 25165824 | bytes 8651776 | tf_op jit(solution)/shard_map/jh,jhpn->hpn/dot_general | solution.py:67
  256.1 8.8 %fusion.36 = f32[8,1,64,128]{3,1,2,0:T(1,128)S(1)} fusion(f32[32,8,1,1]{0,2,3,1:T(1,128)S(1)} %copy.101, f32[32,8,64,128]{3,2,1,0:T(8,128)S(1)} %bitcast.184), kind=kOutput, calls=%fused_computation.48 | convolution fusion | flops 25165824 | bytes 8651776 | tf_op jit(solution)/shard_map/jh,jhpn->hpn/dot_general | solution.py:67
  264.8 8.8 %fusion.38 = f32[8,1,64,128]{3,1,2,0:T(1,128)S(1)} fusion(f32[32,8,1,1]{0,2,3,1:T(1,128)S(1)} %copy.99, f32[32,8,64,128]{3,2,1,0:T(8,128)S(1)} %bitcast.185), kind=kOutput, calls=%fused_computation.50 | convolution fusion | flops 25165824 | bytes 8651776 | tf_op jit(solution)/shard_map/jh,jhpn->hpn/dot_general | solution.py:67
  273.7 8.6 %fusion.32 = f32[8,1,64,128]{3,1,2,0:T(1,128)S(1)} fusion(f32[32,8,1,1]{0,2,3,1:T(1,128)S(1)} %copy.105, f32[32,8,64,128]{3,2,1,0:T(8,128)S(1)} %bitcast.186), kind=kOutput, calls=%fused_computation.44 | convolution fusion | flops 25165824 | bytes 8651776 | tf_op jit(solution)/shard_map/jh,jhpn->hpn/dot_general | solution.py:67
  284.7 2.9 fusion.60
  287.6 1.4 copy-done.4
  288.9 5.4 %fusion.49 = f32[2048,8,64]{0,2,1:T(8,128)} fusion(f32[2048,8,64]{0,2,1:T(8,128)S(1)} %copy-done.4, f32[8,64,2048]{2,1,0:T(8,128)S(1)} %fusion.54, f32[8,64,2048]{2,1,0:T(8,128)S(1)} %fusion.56, f32[8,64,2048]{2,1,0:T(8,128)S(1)} %fusion.58, f32[8,64,2048]{2,1,0:T(8,128)} %fusion.60, f32[2048,8,64]{0,2,1:T(8,128)S(1)} %bitcast.188, f32[8]{0:T(128)S(1)} %copy-done.12, ...), kind=kOutput, calls=%fused_computation.64 | convolution fusion | flops 282132480 | bytes 30539808 | tf_op jit(solution)/shard_map/tn,hpn->thp/dot_general | solution.py:76
  294.3 5.5 %copy.91 = f32[2048,512]{1,0:T(8,128)} copy(f32[2048,512]{0,1:T(8,128)} %bitcast.196) | data formatting | bytes 8388608 | tf_op jit(solution)/shard_map/reshape | solution.py:88
  299.8 3.5 multiply_reduce_fusion
  303.3 8.6 %psum.7 = f32[2048]{0:T(1024)S(1)} all-reduce(f32[2048]{0:T(1024)S(1)} %multiply_reduce_fusion), channel_id=1, replica_groups=mesh['ctx'=32,'head'=4] {'head'}, use_global_device_ids=true, to_apply=%region_7.8 | all-reduce | flops 2048 | bytes 16384 | tf_op jit(solution)/shard_map/psum | solution.py:128
  311.9 3.1 multiply_convert_fusion.3
  315.1 1.3 copy-done.6
  316.4 9.4 %convolution_bitcast_fusion.1 = f32[2048,512]{0,1:T(8,128)} fusion(bf16[2048,512]{1,0:T(8,128)(2,1)S(1)} %multiply_convert_fusion.3, bf16[2048,2048]{1,0:T(8,128)(2,1)} %param.24), kind=kOutput, calls=%fused_computation.75 | convolution fusion | flops 4294967296 | bytes 14680064 | tf_op jit(solution)/shard_map/dot_general | solution.py:132
  325.8 5.3 %copy.107 = f32[2048,512]{1,0:T(8,128)} copy(f32[2048,512]{0,1:T(8,128)} %convolution_bitcast_fusion.1) | data formatting | bytes 8388608
  331.2 81.5 %reduce-scatter.4.cloned.1.call-done = f32[64,512]{1,0:T(8,128)} async-done(((f32[2048,512]{1,0:T(8,128)}), f32[64,512]{1,0:T(8,128)}) %reduce-scatter.4.cloned.1.call-update) | async-done | bytes 131088 | tf_op jit(solution)/shard_map/reduce_scatter | solution.py:131
  412.7 1.6 subtract_convert_fusion
  414.4 46.3 %all-gather.5.cloned.1.call-done = bf16[2048,512]{1,0:T(8,128)(2,1)} async-done(((bf16[64,512]{1,0:T(8,128)(2,1)}), bf16[2048,512]{1,0:T(8,128)(2,1)}) %all-gather.5.cloned.1.call-update) | async-done | bytes 2097168 | tf_op jit(solution)/shard_map/all_gather | solution.py:140
  460.7 3.0 copy.143
  (198 shorter events, 47.7 us)
Async XLA Ops:
  7.2 227.5 %all-gather.7.cloned.1.call-start = ((), (), s32[]{:S(2)}) async-start(), calls=%async_computation.2 | async-start | bytes 8650752 | tf_op jit(solution)/shard_map/all_gather | solution.py:123
  18.0 1.0 copy-start.3
  19.0 142.1 %copy-start.13 = (u32[128]{0:T(128)S(1)}, u32[128]{0:T(128)}, u32[]{:S(2)}) copy-start(u32[128]{0:T(128)} %constant.79) | copy-start | bytes 1540
  159.9 0.7 copy-start.2
  160.6 252.1 %reduce-scatter.4.cloned.1.call-start = ((), (), s32[]{:S(2)}) async-start(), calls=%async_computation.3 | async-start | bytes 4325376 | tf_op jit(solution)/shard_map/reduce_scatter | solution.py:131
  229.6 5.0 %copy-start.7 = (f32[8,5,2048]{2,0,1:T(8,128)S(1)}, f32[8,5,2048]{2,0,1:T(8,128)}, u32[]{:S(2)}) copy-start(f32[8,5,2048]{2,0,1:T(8,128)} %param.22) | copy-start | bytes 983044
  234.7 12.7 %copy-start = (f32[256,64,128]{2,1,0:T(8,128)S(1)}, f32[256,64,128]{2,1,0:T(8,128)}, u32[]{:S(2)}) copy-start(f32[256,64,128]{2,1,0:T(8,128)} %all-gather.7.cloned.1.call-done) | copy-start | bytes 25165828
  283.9 3.6 copy-start.1
  284.0 5.0 %copy-start.4 = (f32[2048,8,64]{0,2,1:T(8,128)S(1)}, f32[2048,8,64]{0,2,1:T(8,128)}, u32[]{:S(2)}) copy-start(f32[2048,8,64]{0,2,1:T(8,128)} %reshape.209) | copy-start | bytes 12582916
  284.0 5.0 %copy-start.12 = (f32[8]{0:T(128)S(1)}, f32[8]{0:T(128)}, u32[]{:S(2)}) copy-start(f32[8]{0:T(128)} %param.21) | copy-start | bytes 100
  294.3 5.5 %copy-start.5 = (bf16[2048,512]{1,0:T(8,128)(2,1)S(1)}, bf16[2048,512]{1,0:T(8,128)(2,1)}, u32[]{:S(2)}) copy-start(bf16[2048,512]{1,0:T(8,128)(2,1)} %param.16) | copy-start | bytes 6291460
  299.8 12.1 %copy-start.11 = (f32[512]{0:T(512)S(1)}, f32[512]{0:T(512)}, u32[]{:S(2)}) copy-start(f32[512]{0:T(512)} %param.23) | copy-start | bytes 6148
  315.0 1.3 copy-start.6
  331.1 81.6 %copy-start.8 = (f32[64,512]{1,0:T(8,128)S(1)}, f32[64,512]{1,0:T(8,128)}, u32[]{:S(2)}) copy-start(f32[64,512]{1,0:T(8,128)} %param.25) | copy-start | bytes 393220
  331.1 81.6 %copy-start.9 = (f32[64,512]{1,0:T(8,128)S(1)}, f32[64,512]{1,0:T(8,128)}, u32[]{:S(2)}) copy-start(f32[64,512]{1,0:T(8,128)} %param.27) | copy-start | bytes 393220
  331.1 81.6 %copy-start.10 = (f32[64,512]{1,0:T(8,128)S(1)}, f32[64,512]{1,0:T(8,128)}, u32[]{:S(2)}) copy-start(f32[64,512]{1,0:T(8,128)} %param.26) | copy-start | bytes 393220
  331.2 129.5 %all-gather.5.cloned.1.call-start = ((), (), s32[]{:S(2)}) async-start(), calls=%async_computation.1 | async-start | bytes 2162688 | tf_op jit(solution)/shard_map/all_gather | solution.py:140
Sparse Core Ops, SparseCore 0:
  160.7 56.6 all-gather.6
  331.3 81.3 reduce-scatter.3
  415.6 45.0 all-gather.4
where the time goes:
time: 479 us; the launch traced here: 471 us
  local copies, waits for them, and re-layouts  143 us (30%)
  waiting for transfers between devices  128 us (27%)
  matrix products  92.1 us (19%)
  blocking collectives  74.6 us (16%)
  other arithmetic  17.5 us (4%)
  between operations  15.1 us (3%)
    dynamic_update_slice x16, local copies, waits for them, and re-layouts, block_scan(): lax.scan(advance, start, (decay_blocks, value_blocks, in_blocks, out_bloc...  106 us
    reduce_scatter x1, waiting for transfers between devices, on_device(): lax.psum_scatter(lax.dot_general(cotangent, normed, (((0,), (0,)), ((), (...  81.5 us
    unnamed x1, blocking collectives  66 us
    dot_general x5, matrix products, level_states(): jnp.einsum('jh,jhpn->hpn', factor, all_ends, precision=lax.Precision.HIGH...  47.5 us
    all_gather x1, waiting for transfers between devices, on_device(): weights = lax.all_gather(updated, 'ctx', axis=0, tiled=True)  46.3 us
    unnamed x35, local copies, waits for them, and re-layouts  17.4 us
    dot_general x5, matrix products, finish(): jnp.einsum('tn,hpn->thp', state_out, level_state.astype(jnp.bfloat16), pr...  10.6 us
  transfers between devices with their start and end apart: 3, of which 2 were waited for; matrix products, arithmetic and copies ran while one was open for 2% of the time, Pallas kernels for 0%

commit v1 on v0

v1 whole, which is shorter than its diff:
```python
import jax
import jax.numpy as jnp
from jax import lax
from jax.experimental import pallas as pl
from jax.experimental.pallas import tpu as pltpu
from jax.sharding import PartitionSpec as P

HD = 64
BLK = 256
NB = 8
NH = 8
CH = 512
ST = 128
LEV = 5
INNER = 2048
DM = 2048
F32 = jnp.float32
BF16 = jnp.bfloat16
MESH = pl.DeviceIdType.MESH
DIMS = 4


def nt(a, b):
    return lax.dot_general(a, b, (((1,), (1,)), ((), ())), preferred_element_type=F32)


def nn(a, b):
    return lax.dot_general(a, b, (((1,), (0,)), ((), ())), preferred_element_type=F32)


def flip(y, z, mask):
    if mask & 1:
        z = z + 1 - 2 * lax.rem(z, 2)
    if mask & 2:
        z = 3 - z
    if mask & 4:
        y = y + 1 - 2 * lax.rem(y, 2)
    if mask & 8:
        y = 3 - y
    return y, z


def stream_dims(s):
    return [(s + t) % DIMS for t in range(DIMS)]


def span(dims):
    masks = [0]
    for d in dims:
        masks = masks + [m | (1 << d) for m in masks]
    return masks


SCRATCH = dict(
    xv=pltpu.VMEM((NB, BLK, CH), BF16),
    zv=pltpu.VMEM((NB, BLK, CH), BF16),
    bv=pltpu.VMEM((NB, BLK, ST), BF16),
    cv=pltpu.VMEM((NB, BLK, ST), BF16),
    dtv=pltpu.VMEM((NH, NB * BLK), F32),
    gatev=pltpu.VMEM((LEV, NH, NB * BLK), F32),
    ngv=pltpu.VMEM((1, CH), F32),
    gcol=pltpu.VMEM((CH, 128), F32),
    xt=pltpu.VMEM((NB, CH, BLK), BF16),
    xa=pltpu.VMEM((NB, CH, BLK), BF16),
    runs=pltpu.VMEM((NB, CH, ST), BF16),
    run=pltpu.VMEM((CH, ST), F32),
    acc=pltpu.VMEM((NB, CH, BLK), F32),
    sil=pltpu.VMEM((NB, CH, BLK), F32),
    ep=pltpu.VMEM((NB, NH, BLK), F32),
    e1=pltpu.VMEM((NB, NH, BLK), F32),
    ecum=pltpu.VMEM((NB, NH, BLK), F32),
    ebuf=pltpu.VMEM((2, CH, ST), F32),
    dbuf=pltpu.VMEM((2, NH, 128), F32),
    sz=pltpu.VMEM((4, CH // 2, ST), F32),
    dz=pltpu.VMEM((4, NH, 128), F32),
    sy=pltpu.VMEM((4, CH // 2, ST), BF16),
    dy=pltpu.VMEM((4, NH, 128), F32),
    lev=pltpu.VMEM((LEV, CH, ST), BF16),
    fac=pltpu.VMEM((LEV, NH, BLK), F32),
    ssb=pltpu.VMEM((4, NB, 8, BLK), F32),
    nt_=pltpu.VMEM((CH, NB * BLK), BF16),
    cotv=pltpu.VMEM((NB * BLK, DM), BF16),
    gsend=pltpu.VMEM((8, 256, 256), BF16),
    gown=pltpu.VMEM((8, 256, 256), F32),
    grecv=pltpu.VMEM((8, 256, 256), BF16),
    part=pltpu.VMEM((16, 256, 128), F32),
    sb=pltpu.VMEM((4, 15, HD, 128), BF16),
    r0=pltpu.VMEM((4, 8, HD, 128), BF16),
    r1=pltpu.VMEM((4, 4, HD, 128), BF16),
    r2=pltpu.VMEM((4, 2, HD, 128), BF16),
    r3=pltpu.VMEM((4, 1, HD, 128), BF16),
    gt=pltpu.VMEM((128, 256), F32),
    gx=pltpu.VMEM((64, 256), F32),
    mw=pltpu.VMEM((3, 128, 256), F32),
    w=pltpu.VMEM((16, 2, 128, 256), BF16),
    s_x=pltpu.SemaphoreType.DMA((NB,)),
    s_z=pltpu.SemaphoreType.DMA((NB,)),
    s_in=pltpu.SemaphoreType.DMA((6,)),
    s_n=pltpu.SemaphoreType.DMA((NB,)),
    s_out=pltpu.SemaphoreType.DMA((4,)),
    s_m=pltpu.SemaphoreType.DMA((3,)),
    e_s=pltpu.SemaphoreType.DMA((2,)),
    e_r=pltpu.SemaphoreType.DMA((2,)),
    z_s=pltpu.SemaphoreType.DMA((3, 2)),
    z_r=pltpu.SemaphoreType.DMA((3, 2)),
    y_s=pltpu.SemaphoreType.DMA((3, 2)),
    y_r=pltpu.SemaphoreType.DMA((3, 2)),
    l_s=pltpu.SemaphoreType.DMA((4,)),
    l_r=pltpu.SemaphoreType.DMA((4,)),
    q_s=pltpu.SemaphoreType.DMA((NB, 3)),
    q_r=pltpu.SemaphoreType.DMA((NB, 3)),
    m_s=pltpu.SemaphoreType.DMA((3,)),
    m_r=pltpu.SemaphoreType.DMA((3,)),
    p_s=pltpu.SemaphoreType.DMA((8,)),
    p_r=pltpu.SemaphoreType.DMA((8,)),
    r_s=pltpu.SemaphoreType.DMA((4, 15)),
    r_r=pltpu.SemaphoreType.DMA((4, 15)),
    g_s=pltpu.SemaphoreType.DMA((1,)),
    g_r=pltpu.SemaphoreType.DMA((1,)),
    a_s=pltpu.SemaphoreType.DMA((4, 15)),
    a_r=pltpu.SemaphoreType.DMA((4, 15)),
    c_s=pltpu.SemaphoreType.DMA((4, 16)),
    c_r=pltpu.SemaphoreType.DMA((4, 16)),
)


class Refs:
    pass


def kernel(
    x_h, z_h, b_h, c_h, dt_h, dr_s, sk_s, gate_h, ng_h, cot_h, mw_h, m1_h, m2_h,
    n_out, w_out, g_out, *scratch,
):
    v = Refs()
    for name, ref in zip(SCRATCH, scratch):
        setattr(v, name, ref)
    ctx = lax.axis_index("ctx")
    head = lax.axis_index("head")
    core = lax.rem(ctx, 2)
    z = lax.rem(ctx // 2, 4)
    y = ctx // 8
    half = pl.multiple_of(core * 256, 256)
    other = pl.multiple_of((1 - core) * 256, 256)

    def at(yy, zz, cc):
        return ((yy * 4 + zz) * 2 + cc, head)

    partner = at(y, z, 1 - core)
    zpeers = [at(y, lax.rem(z + d, 4), core) for d in (1, 2, 3)]
    ypeers = [at(lax.rem(y + d, 4), z, core) for d in (1, 2, 3)]
    xpeers = [(ctx, lax.rem(head + d, 4)) for d in (1, 2, 3)]
    cube = []
    for d in range(DIMS):
        yy, zz = flip(y, z, 1 << d)
        cube.append(at(yy, zz, core))

    def remote(src, dst, ssem, rsem, dev):
        return pltpu.make_async_remote_copy(
            src_ref=src, dst_ref=dst, send_sem=ssem, recv_sem=rsem, device_id=dev, device_id_type=MESH
        )

    barrier = pltpu.get_barrier_semaphore()
    for dev in [partner] + zpeers + ypeers + xpeers:
        pl.semaphore_signal(barrier, inc=1, device_id=dev, device_id_type=MESH)

    def load_x(b):
        return pltpu.make_async_copy(x_h.at[pl.ds(b * BLK, BLK)], v.xv.at[b], v.s_x.at[b])

    def load_z(b):
        return pltpu.make_async_copy(z_h.at[pl.ds(b * BLK, BLK)], v.zv.at[b], v.s_z.at[b])

    ld_dt = pltpu.make_async_copy(dt_h, v.dtv, v.s_in.at[0])
    ld_b = pltpu.make_async_copy(b_h, v.bv, v.s_in.at[1])
    ld_c = pltpu.make_async_copy(c_h, v.cv, v.s_in.at[2])
    ld_g = pltpu.make_async_copy(gate_h, v.gatev, v.s_in.at[3])
    ld_n = pltpu.make_async_copy(ng_h, v.ngv, v.s_in.at[4])
    ld_cot = pltpu.make_async_copy(cot_h, v.cotv, v.s_in.at[5])
    ld_dt.start()
    load_x(0).start()
    ld_b.start()
    for b in range(1, NB):
        load_x(b).start()
    ld_c.start()
    for b in range(NB):
        load_z(b).start()
    ld_g.start()
    ld_n.start()
    ld_cot.start()
    moments = (mw_h, m1_h, m2_h)
    ld_m = [
        pltpu.make_async_copy(
            ref.at[:, pl.ds(half, 256)],
            v.mw.at[k, pl.ds(pl.multiple_of(core * 64, 64), 64)],
            v.s_m.at[k],
        )
        for k, ref in enumerate(moments)
    ]
    for cp in ld_m:
        cp.start()
    ex_m = [
        remote(
            ref.at[:, pl.ds(other, 256)],
            v.mw.at[k, pl.ds(pl.multiple_of(core * 64, 64), 64)],
            v.m_s.at[k],
            v.m_r.at[k],
            partner,
        )
        for k, ref in enumerate(moments)
    ]

    iota_h = lax.broadcasted_iota(jnp.int32, (NH, 128), 0)
    rate = jnp.zeros((NH, 128), F32)
    for h in range(NH):
        rate = jnp.where(iota_h == h, dr_s[h], rate)
    row = lax.broadcasted_iota(jnp.int32, (BLK, BLK), 0)
    col = lax.broadcasted_iota(jnp.int32, (BLK, BLK), 1)
    upper = (row <= col).astype(F32)
    rate2 = jnp.concatenate([rate, rate], axis=1)
    v.run[...] = jnp.zeros_like(v.run)
    ld_dt.wait()

    def hs(h):
        return slice(h * HD, (h + 1) * HD)

    def a1(b, off):
        dt = v.dtv[:, pl.ds(pl.multiple_of(b * BLK, BLK), BLK)]
        ld = -rate2 * dt
        prefix = lax.dot_general(
            ld, upper, (((1,), (0,)), ((), ())), precision=lax.Precision.HIGHEST, preferred_element_type=F32
        )
        total = jnp.broadcast_to(prefix[:, BLK - 1 :], (NH, BLK))
        tail = jnp.exp(total - prefix)
        v.ep[b] = jnp.exp(prefix)
        v.e1[b] = jnp.exp(prefix - total)
        v.ecum[b] = jnp.exp(off + prefix)
        load_x(b).wait()
        xt = v.xv[b].T
        v.xt[b] = xt
        for h in range(NH):
            scaled = (xt[hs(h)].astype(F32) * dt[h : h + 1]).astype(BF16)
            v.xa[b, hs(h)] = (scaled.astype(F32) * tail[h : h + 1]).astype(BF16)
        upd = nn(v.xa[b], v.bv[b])
        et = jnp.exp(total[:, :128])
        for h in range(NH):
            old = v.run[hs(h)]
            v.runs[b, hs(h)] = old.astype(BF16)
            v.run[hs(h)] = old * et[h : h + 1] + upd[hs(h)]
        return off + total

    ld_b.wait()
    dsum = lax.fori_loop(0, NB, a1, jnp.zeros((NH, BLK), F32))
    v.ebuf[core] = v.run[...]
    v.dbuf[core] = dsum[:, :128]

    pl.semaphore_wait(barrier, 10)
    ex_e = [
        remote(v.ebuf.at[core], v.ebuf.at[core], v.e_s.at[0], v.e_r.at[0], partner),
        remote(v.dbuf.at[core], v.dbuf.at[core], v.e_s.at[1], v.e_r.at[1], partner),
    ]
    for cp in ex_e:
        cp.start()
    for cp in ex_m:
        cp.start()

    ld_c.wait()
    causal = row <= col

    def a2(b, carry):
        c_b = v.cv[b]
        scores = jnp.where(causal, nt(v.bv[b], c_b), 0.0).astype(BF16)
        local = nn(v.xa[b], scores)
        carried = nt(v.runs[b], c_b)
        for h in range(NH):
            v.acc[b, hs(h)] = local[hs(h)] * v.e1[b, h : h + 1] + carried[hs(h)] * v.ep[b, h : h + 1]
        load_z(b).wait()
        zt = v.zv[b].T
        for h in range(NH):
            zz = zt[hs(h)].astype(F32)
            v.sil[b, hs(h)] = zz / (1.0 + jnp.exp(-zz))
        return carry

    lax.fori_loop(0, 2, a2, 0)

    for cp in ex_e:
        cp.wait()
    d0, d1 = v.dbuf[0], v.dbuf[1]
    v.dz[z] = d0 + d1
    dpre = jnp.where(core == 1, d0, 0.0)

    def hrow(ref, k, j):
        return jnp.exp(ref[k, pl.ds(core * 4 + j, 1)])

    for j in range(4):
        rows = pl.ds(pl.multiple_of(half + j * HD, HD), HD)
        v.sz[z, hs(j)] = v.ebuf[0, rows] * hrow(v.dbuf, 1, j) + v.ebuf[1, rows]
    ex_z = []
    for d in range(3):
        ex_z.append(remote(v.sz.at[z], v.sz.at[z], v.z_s.at[d, 0], v.z_r.at[d, 0], zpeers[d]))
        ex_z.append(remote(v.dz.at[z], v.dz.at[z], v.z_s.at[d, 1], v.z_r.at[d, 1], zpeers[d]))
    for cp in ex_z:
        cp.start()
    lax.fori_loop(2, 6, a2, 0)

    for cp in ex_z:
        cp.wait()
    v.dy[y] = (v.dz[0] + v.dz[1]) + (v.dz[2] + v.dz[3])
    zpre = dpre
    for k in range(3):
        zpre = zpre + jnp.where(z > k, v.dz[k], 0.0)
    zflip = z + 1 - 2 * lax.rem(z, 2)
    for j in range(4):
        s01 = v.sz[0, hs(j)] * hrow(v.dz, 1, j) + v.sz[1, hs(j)]
        s012 = s01 * hrow(v.dz, 2, j) + v.sz[2, hs(j)]
        v.sy[y, hs(j)] = (s012 * hrow(v.dz, 3, j) + v.sz[3, hs(j)]).astype(BF16)
        rows = pl.ds(pl.multiple_of(half + j * HD, HD), HD)
        v.lev[1, rows] = v.sz[zflip, hs(j)].astype(BF16)
        v.lev[2, rows] = s01.astype(BF16)
    ex_y = []
    for d in range(3):
        ex_y.append(remote(v.sy.at[y], v.sy.at[y], v.y_s.at[d, 0], v.y_r.at[d, 0], ypeers[d]))
        ex_y.append(remote(v.dy.at[y], v.dy.at[y], v.y_s.at[d, 1], v.y_r.at[d, 1], ypeers[d]))
    for cp in ex_y:
        cp.start()

    def swap(level):
        piece = v.lev.at[level, pl.ds(half, 256)]
        return remote(piece, piece, v.l_s.at[level - 1], v.l_r.at[level - 1], partner)

    for level in (1, 2):
        swap(level).start()
    v.lev[0] = v.ebuf[0].astype(BF16)

    def set_factor(level, value):
        v.fac[level] = jnp.concatenate([value, value], axis=1)

    set_factor(0, jnp.full((NH, 128), jnp.where(core == 1, 1.0, 0.0), F32))
    set_factor(1, jnp.where(lax.rem(z, 2) == 1, jnp.exp(dpre), 0.0))
    set_factor(2, jnp.where(z >= 2, jnp.exp(dpre + jnp.where(z == 3, v.dz[2], 0.0)), 0.0))
    lax.fori_loop(6, 8, a2, 0)
    ld_g.wait()
    for level in (1, 2):
        swap(level).wait()

    def scaled_gate(b, level):
        lanes = pl.ds(pl.multiple_of(b * BLK, BLK), BLK)
        return v.gatev[level, :, lanes] * (v.fac[level] * v.ecum[b])

    def b1(b, carry):
        c_b = v.cv[b]
        reads = [nt(v.lev[level], c_b) for level in range(3)]
        gates = [scaled_gate(b, level) for level in range(3)]
        for h in range(NH):
            add = reads[0][hs(h)] * gates[0][h : h + 1]
            for level in (1, 2):
                add = add + reads[level][hs(h)] * gates[level][h : h + 1]
            v.acc[b, hs(h)] = v.acc[b, hs(h)] + add
        return carry

    lax.fori_loop(0, 5, b1, 0)

    for cp in ex_y:
        cp.wait()
    yflip = y + 1 - 2 * lax.rem(y, 2)
    for j in range(4):
        s01 = v.sy[0, hs(j)].astype(F32) * hrow(v.dy, 1, j) + v.sy[1, hs(j)].astype(F32)
        rows = pl.ds(pl.multiple_of(half + j * HD, HD), HD)
        v.lev[3, rows] = v.sy[yflip, hs(j)]
        v.lev[4, rows] = s01.astype(BF16)
    for level in (3, 4):
        swap(level).start()
    set_factor(3, jnp.where(lax.rem(y, 2) == 1, jnp.exp(zpre), 0.0))
    set_factor(4, jnp.where(y >= 2, jnp.exp(zpre + jnp.where(y == 3, v.dy[2], 0.0)), 0.0))
    lax.fori_loop(5, 8, b1, 0)
    ld_n.wait()
    v.gcol[...] = jnp.broadcast_to(v.ngv[...], (128, CH)).T
    for level in (3, 4):
        swap(level).wait()

    def ex_q(b, d):
        piece = v.ssb.at[head, b]
        return remote(piece, piece, v.q_s.at[b, d], v.q_r.at[b, d], xpeers[d])

    def b2(b, carry):
        c_b = v.cv[b]
        reads = [nt(v.lev[level], c_b) for level in (3, 4)]
        gates = [scaled_gate(b, level) for level in (3, 4)]
        squares = jnp.zeros((8, BLK), F32)
        for h in range(NH):
            inside = v.acc[b, hs(h)] + reads[0][hs(h)] * gates[0][h : h + 1] + reads[1][hs(h)] * gates[1][h : h + 1]
            mixed = inside + v.xt[b, hs(h)].astype(F32) * sk_s[h]
            gated = mixed * v.sil[b, hs(h)]
            v.acc[b, hs(h)] = gated
            squares = squares + jnp.sum((gated * gated).reshape(8, 8, BLK), axis=0)
        v.ssb[head, b] = squares
        for d in range(3):
            ex_q(b, d).start()
        return carry

    def b3(b, carry):
        for d in range(3):
            ex_q(b, d).wait()
        total = (v.ssb[0, b] + v.ssb[1, b]) + (v.ssb[2, b] + v.ssb[3, b])
        r = lax.rsqrt(jnp.sum(total, axis=0, keepdims=True) / INNER + 1e-05)
        lanes = pl.ds(pl.multiple_of(b * BLK, BLK), BLK)
        for h in range(NH):
            gain = v.gcol[hs(h)]
            n = v.acc[b, hs(h)] * r * jnp.concatenate([gain, gain], axis=1)
            v.nt_[hs(h), lanes] = n.astype(BF16)
        v.xv[b] = v.nt_[:, lanes].T
        pltpu.make_async_copy(v.xv.at[b], n_out.at[pl.ds(b * BLK, BLK)], v.s_n.at[b]).start()
        return carry

    lax.fori_loop(0, NB, b2, 0)
    lax.fori_loop(0, NB, b3, 0)

    ld_cot.wait()
    def ex_p(p):
        return remote(v.gsend.at[p], v.grecv.at[p], v.p_s.at[p], v.p_r.at[p], partner)

    recv_bufs = (v.r0, v.r1, v.r2, v.r3)
    starts = (0, 8, 12, 14)

    def sent_masks(s, t):
        dims = stream_dims(s)
        return [m | (1 << dims[t]) for m in span(dims[t + 1 :])]

    def ex_r(s, t, i):
        dims = stream_dims(s)
        k = starts[t] + i
        return remote(v.sb.at[s, k], recv_bufs[t].at[s, i], v.r_s.at[s, k], v.r_r.at[s, k], cube[dims[t]])

    def finish_pair(p):
        ex_p(p).wait()
        for a in range(2):
            lanes = slice(a * 128, (a + 1) * 128)
            m = 2 * p + a
            total = v.gown[p, :, lanes] + v.grecv[p, :, lanes].astype(F32)
            for s in range(4):
                if m >> s & 1:
                    v.sb[s, sent_masks(s, 0).index(m)] = total[hs(s)].astype(BF16)
                else:
                    v.part[m, hs(s)] = total[hs(s)]
        for s in range(4):
            for i, m in enumerate(sent_masks(s, 0)):
                if m >> 1 == p:
                    ex_r(s, 0, i).start()

    for p in range(7, -1, -1):
        sides = []
        for m in (2 * p, 2 * p + 1):
            yy, zz = flip(y, z, m)
            sides.append(v.cotv[:, pl.ds(pl.multiple_of((yy * 4 + zz) * 128, 128), 128)])
        cot = jnp.concatenate(sides, axis=1)
        v.gsend[p] = nn(v.nt_[pl.ds(other, 256), :], cot).astype(BF16)
        ex_p(p).start()
        v.gown[p] = nn(v.nt_[pl.ds(half, 256), :], cot)
        if p < 7:
            finish_pair(p + 1)
    finish_pair(0)

    for t in range(3):
        for s in range(4):
            dims = stream_dims(s)
            kept = span(dims[t + 1 :])
            nxt = sent_masks(s, t + 1)
            for i, m in enumerate(kept):
                ex_r(s, t, i).wait()
                total = v.part[m, hs(s)] + recv_bufs[t][s, i].astype(F32)
                if m in nxt:
                    k = nxt.index(m)
                    v.sb[s, starts[t + 1] + k] = total.astype(BF16)
                    ex_r(s, t + 1, k).start()
                else:
                    v.part[m, hs(s)] = total
    for s in range(4):
        ex_r(s, 3, 0).wait()
        v.gt[:, hs(s)] = (v.part[0, hs(s)] + v.r3[s, 0].astype(F32)).T

    ex_g = remote(
        v.gt.at[pl.ds(pl.multiple_of((1 - core) * 64, 64), 64)], v.gx, v.g_s.at[0], v.g_r.at[0], partner
    )
    ex_g.start()
    for cp in ld_m:
        cp.wait()
    for cp in ex_m:
        cp.wait()
    own = y * 4 + z
    grad = v.gt[...]
    one = 0.9 * v.mw[1] + 0.1 * grad
    two = 0.95 * v.mw[2] + 0.05 * grad * grad
    ratio = one / (1.0 - 0.9**10) / (jnp.sqrt(two / (1.0 - 0.95**10)) + 1e-08)
    master = v.mw[0]
    v.w[own, core] = (master - 0.1 * (ratio + 0.1 * master)).astype(BF16)

    def slot(m):
        yy, zz = flip(y, z, m)
        return yy * 4 + zz

    def ex_a(s, t, i):
        dims = stream_dims(s)
        m = span(dims[:t])[i]
        piece = v.w.at[slot(m), core, pl.ds(s * 32, 32)]
        k = (1 << t) - 1 + i
        return remote(piece, piece, v.a_s.at[s, k], v.a_r.at[s, k], cube[dims[t]])

    def ex_c(s, i):
        m = span(stream_dims(s))[i]
        piece = v.w.at[slot(m), core, pl.ds(s * 32, 32)]
        return remote(piece, piece, v.c_s.at[s, i], v.c_r.at[s, i], partner)

    for t in range(4):
        for s in range(4):
            ex_a(s, t, 0).start()
    for s in range(4):
        ex_c(s, 0).start()
    for t in range(4):
        for i in range(1 << t):
            for s in range(4):
                ex_a(s, t, i).wait_recv()
                got = (1 << t) + i
                for later in range(t + 1, 4):
                    ex_a(s, later, got).start()
                ex_c(s, got).start()
    ex_g.wait()
    mine = pl.ds(pl.multiple_of(core * 64, 64), 64)
    outs = [
        pltpu.make_async_copy(v.gt.at[mine], g_out.at[:, pl.ds(half, 256)], v.s_out.at[0]),
        pltpu.make_async_copy(v.gx, g_out.at[:, pl.ds(other, 256)], v.s_out.at[1]),
        pltpu.make_async_copy(v.w.at[:, core], w_out.at[:, :, pl.ds(half, 256)], v.s_out.at[2]),
    ]
    for cp in outs:
        cp.start()
    for s in range(4):
        for i in range(16):
            ex_c(s, i).wait()
    last = pltpu.make_async_copy(v.w.at[:, 1 - core], w_out.at[:, :, pl.ds(other, 256)], v.s_out.at[3])
    last.start()
    for s in range(4):
        for t in range(4):
            for i in range(1 << t):
                ex_a(s, t, i).wait_send()
    for b in range(NB):
        pltpu.make_async_copy(v.xv.at[b], n_out.at[pl.ds(b * BLK, BLK)], v.s_n.at[b]).wait()
    for cp in outs:
        cp.wait()
    last.wait()


def on_device(
    entries, gating, state_in, state_out, step_size, decay_rate, skip_gain, level_gate,
    norm_gain, cotangent, master_weight, first_moment, second_moment,
):
    anyspace = pl.BlockSpec(memory_space=pl.ANY)
    smem = pl.BlockSpec(memory_space=pltpu.SMEM)
    normed, weights, gradient = pl.pallas_call(
        kernel,
        out_shape=(
            jax.ShapeDtypeStruct((NB * BLK, CH), BF16),
            jax.ShapeDtypeStruct((16, 128, CH), BF16),
            jax.ShapeDtypeStruct((64, CH), F32),
        ),
        in_specs=[anyspace] * 5 + [smem] * 2 + [anyspace] * 6,
        out_specs=(anyspace,) * 3,
        scratch_shapes=list(SCRATCH.values()),
        compiler_params=pltpu.CompilerParams(
            collective_id=0, has_side_effects=True, vmem_limit_bytes=60 * 1024 * 1024
        ),
    )(
        entries,
        gating,
        state_in.reshape(NB, BLK, ST),
        state_out.reshape(NB, BLK, ST),
        step_size,
        decay_rate,
        skip_gain,
        level_gate.transpose(1, 0, 2),
        norm_gain.reshape(1, CH),
        cotangent,
        master_weight,
        first_moment,
        second_moment,
    )
    return normed, weights.reshape(DM, CH), gradient


def solution(mesh):
    return jax.shard_map(
        on_device,
        mesh=mesh,
        in_specs=(
            P("ctx", "head"),
            P("ctx", "head"),
            P("ctx", None),
            P("ctx", None),
            P("head", "ctx"),
            P("head"),
            P("head"),
            P("head", None, "ctx"),
            P("head"),
            P("ctx", None),
            P("ctx", "head"),
            P("ctx", "head"),
            P("ctx", "head"),
        ),
        out_specs=(P("ctx", "head"), P(None, "head"), P("ctx", "head")),
        check_vma=False,
    )
```

time: 479 us -> 86.8 us (0.18); the launches traced: 471 us -> 86.7 us
  local copies, waits for them, and re-layouts: 143 us -> 5.18 us
  waiting for transfers between devices: 128 us -> 0 us
  matrix products: 92.1 us -> 0 us
  Pallas kernels: 0 us -> 80.9 us
  blocking collectives: 74.6 us -> 0 us
  other arithmetic: 17.5 us -> 0 us
  between operations: 15.1 us -> 0.65 us
    dynamic_update_slice x16 -> x0, local copies, waits for them, and re-layouts: 106 us -> none  [block_scan(): lax.scan(advance, start, (decay_blocks, value_blocks, in_blocks, out_bloc...]
    dot_general x43 -> x0, matrix products: 92.1 us -> none  [the longest x5 47.5 us: level_states(): jnp.einsum('jh,jhpn->hpn', factor, all_ends, precision=lax.Precision.HIGH...]
    reduce_scatter x1 -> x0, waiting for transfers between devices: 81.5 us -> none  [on_device(): lax.psum_scatter(lax.dot_general(cotangent, normed, (((0,), (0,)), ((), (...]
    pallas_call x0 -> x1, Pallas kernels: none -> 80.9 us  [on_device(): pl.pallas_call(kernel, out_shape=(jax.ShapeDtypeStruct((NB * BLK, CH), BF...]
    unnamed x1 -> x0, blocking collectives: 66 us -> none
    all_gather x2 -> x0, waiting for transfers between devices: 46.3 us -> none  [the longest x1 46.3 us: on_device(): weights = lax.all_gather(updated, 'ctx', axis=0, tiled=True)]
    unnamed x35 -> x7, local copies, waits for them, and re-layouts: 17.4 us -> 5.18 us
    reshape x10 -> x0, local copies, waits for them, and re-layouts: 10.5 us -> none  [the longest x1 5.49 us: finish(): mixed.reshape(length, head_count * head_width)]
  transfers between devices with their start and end apart: 3 -> 0, of which waited for: 2 -> 0; matrix products, arithmetic and copies ran while one was open for 2% -> 0% of each run, Pallas kernels for 0% -> 0%
where the time goes in v1:
time: 86.8 us; the launch traced here: 86.7 us
  Pallas kernels  80.9 us (93%)
  local copies, waits for them, and re-layouts  5.18 us (6%)
    pallas_call x1, Pallas kernels, on_device(): pl.pallas_call(kernel, out_shape=(jax.ShapeDtypeStruct((NB * BLK, CH), BF...  80.9 us
    unnamed x7, local copies, waits for them, and re-layouts  5.18 us

profile of v1, /device:TPU:1, one launch (start us, length us, event | category | flops | bytes accessed | tf_op | source)
XLA Modules:
  0.0 86.7 jit_solution(10629298839704509114)
XLA Ops:
  0.6 80.9 %shard_map.148 = (bf16[2048,512]{1,0:T(8,128)(2,1)}, bf16[16,128,512]{2,1,0:T(8,128)(2,1)}, f32[64,512]{1,0:T(8,128)}) custom-call(bf16[2048,512]{1,0:T(8,128)(2,1)} %x_h.1, bf16[2048,512]{1,0:T(8,128)(2,1)} %z_h.1, bf16[8,256,128]{2,1,0:T(8,128)(2,1)} %bitcast.6, bf16[8,256,128]{2,1,0:T(8,128)(2,1)} %bitcast.7, f32[8,2048]{1,0:T(8,128)} %dt_h.1, f32[8]{0:T(128)} %dr_s.1, ...), custom_call_target="tpu_custom_call" | custom-call | tf_op jit(solution)/shard_map/pallas_call | solution.py:556
  81.5 0.0 copy-start
  81.5 3.2 %copy.19 = bf16[2048,512]{1,0:T(8,128)(2,1)} copy(bf16[2048,512]{1,0:T(8,128)(2,1)} %get-tuple-element.12) | data formatting | bytes 4194304
  84.7 0.0 copy-done
  84.7 0.0 copy-start.1
  84.7 1.3 %copy.20 = bf16[2048,512]{1,0:T(8,128)(2,1)} copy(bf16[2048,512]{1,0:T(8,128)(2,1)S(1)} %bitcast.5) | data formatting | bytes 4194304
  86.0 0.0 copy-done.1
  86.0 0.7 copy.21
Async XLA Ops:
  81.5 3.2 %copy-start = (bf16[16,128,512]{2,1,0:T(8,128)(2,1)S(1)}, bf16[16,128,512]{2,1,0:T(8,128)(2,1)}, u32[]{:S(2)}) copy-start(bf16[16,128,512]{2,1,0:T(8,128)(2,1)} %get-tuple-element.7) | copy-start | bytes 6291460
  84.7 1.3 %copy-start.1 = (f32[64,512]{1,0:T(8,128)S(1)}, f32[64,512]{1,0:T(8,128)}, u32[]{:S(2)}) copy-start(f32[64,512]{1,0:T(8,128)} %get-tuple-element.14) | copy-start | bytes 393220

commit v2 on v1

--- a/solution.py
+++ b/solution.py
@@ -51,8 +51,32 @@
     return masks
 
 
+LAG = 2
+HOP = 3
+
+
+def schedule_events():
+    out = []
+    for s in range(4):
+        dims = stream_dims(s)
+        sent = {}
+        done = {m: 7 - (m >> 1) + LAG for m in range(16)}
+        for m in range(16):
+            if m >> dims[0] & 1:
+                sent[m] = done[m]
+        for t in range(3):
+            for i, m in enumerate(span(dims[t + 1 :])):
+                when = max(sent[m | 1 << dims[t]] + HOP, done[m])
+                done[m] = when
+                out.append((when, s, t, i))
+                if m >> dims[t + 1] & 1:
+                    sent[m] = when
+    return sorted(out, key=lambda e: (e[0], e[2], e[3], e[1]))
+
+
 SCRATCH = dict(
     xv=pltpu.VMEM((NB, BLK, CH), BF16),
+    pre=pltpu.VMEM((NB, NH, BLK), F32),
     zv=pltpu.VMEM((NB, BLK, CH), BF16),
     bv=pltpu.VMEM((NB, BLK, ST), BF16),
     cv=pltpu.VMEM((NB, BLK, ST), BF16),
@@ -71,13 +95,13 @@
     ecum=pltpu.VMEM((NB, NH, BLK), F32),
     ebuf=pltpu.VMEM((2, CH, ST), F32),
     dbuf=pltpu.VMEM((2, NH, 128), F32),
-    sz=pltpu.VMEM((4, CH // 2, ST), F32),
+    sz=pltpu.VMEM((4, CH // 2, ST), BF16),
     dz=pltpu.VMEM((4, NH, 128), F32),
     sy=pltpu.VMEM((4, CH // 2, ST), BF16),
     dy=pltpu.VMEM((4, NH, 128), F32),
     lev=pltpu.VMEM((LEV, CH, ST), BF16),
     fac=pltpu.VMEM((LEV, NH, BLK), F32),
-    ssb=pltpu.VMEM((4, NB, 8, BLK), F32),
+    ssb=pltpu.VMEM((4, NB, 1, BLK), F32),
     nt_=pltpu.VMEM((CH, NB * BLK), BF16),
     cotv=pltpu.VMEM((NB * BLK, DM), BF16),
     gsend=pltpu.VMEM((8, 256, 256), BF16),
@@ -90,14 +114,10 @@
     r2=pltpu.VMEM((4, 2, HD, 128), BF16),
     r3=pltpu.VMEM((4, 1, HD, 128), BF16),
     gt=pltpu.VMEM((128, 256), F32),
-    gx=pltpu.VMEM((64, 256), F32),
     mw=pltpu.VMEM((3, 128, 256), F32),
-    w=pltpu.VMEM((16, 2, 128, 256), BF16),
     s_x=pltpu.SemaphoreType.DMA((NB,)),
     s_z=pltpu.SemaphoreType.DMA((NB,)),
     s_in=pltpu.SemaphoreType.DMA((6,)),
-    s_n=pltpu.SemaphoreType.DMA((NB,)),
-    s_out=pltpu.SemaphoreType.DMA((4,)),
     s_m=pltpu.SemaphoreType.DMA((3,)),
     e_s=pltpu.SemaphoreType.DMA((2,)),
     e_r=pltpu.SemaphoreType.DMA((2,)),
@@ -130,11 +150,12 @@
 
 def kernel(
     x_h, z_h, b_h, c_h, dt_h, dr_s, sk_s, gate_h, ng_h, cot_h, mw_h, m1_h, m2_h,
-    n_out, w_out, g_out, *scratch,
+    n_out, w_out, gt_out, gx_out, *scratch,
 ):
     v = Refs()
     for name, ref in zip(SCRATCH, scratch):
         setattr(v, name, ref)
+    v.w, v.gx = w_out, gx_out
     ctx = lax.axis_index("ctx")
     head = lax.axis_index("head")
     core = lax.rem(ctx, 2)
@@ -220,21 +241,38 @@
     v.run[...] = jnp.zeros_like(v.run)
     ld_dt.wait()
 
+    def pairs(lo, hi, body, before=None, after=None, carry=0):
+        def trip(j, carry):
+            two = (lo + 2 * j, lo + 2 * j + 1)
+            if before is not None:
+                for b in two:
+                    before(b)
+            for b in two:
+                carry = body(b, carry)
+            if after is not None:
+                for b in two:
+                    after(b)
+            return carry
+
+        return lax.fori_loop(0, (hi - lo) // 2, trip, carry)
+
     def hs(h):
         return slice(h * HD, (h + 1) * HD)
 
+    logs = jnp.concatenate([-rate2 * v.dtv[:, b * BLK : (b + 1) * BLK] for b in range(NB)], axis=0)
+    prefixes = lax.dot_general(
+        logs, upper, (((1,), (0,)), ((), ())), precision=lax.Precision.HIGHEST, preferred_element_type=F32
+    )
+    v.pre[...] = prefixes.reshape(NB, NH, BLK)
+
     def a1(b, off):
         dt = v.dtv[:, pl.ds(pl.multiple_of(b * BLK, BLK), BLK)]
-        ld = -rate2 * dt
-        prefix = lax.dot_general(
-            ld, upper, (((1,), (0,)), ((), ())), precision=lax.Precision.HIGHEST, preferred_element_type=F32
-        )
+        prefix = v.pre[b]
         total = jnp.broadcast_to(prefix[:, BLK - 1 :], (NH, BLK))
         tail = jnp.exp(total - prefix)
         v.ep[b] = jnp.exp(prefix)
         v.e1[b] = jnp.exp(prefix - total)
         v.ecum[b] = jnp.exp(off + prefix)
-        load_x(b).wait()
         xt = v.xv[b].T
         v.xt[b] = xt
         for h in range(NH):
@@ -249,7 +287,7 @@
         return off + total
 
     ld_b.wait()
-    dsum = lax.fori_loop(0, NB, a1, jnp.zeros((NH, BLK), F32))
+    dsum = pairs(0, NB, a1, before=lambda b: load_x(b).wait(), carry=jnp.zeros((NH, BLK), F32))
     v.ebuf[core] = v.run[...]
     v.dbuf[core] = dsum[:, :128]
 
@@ -273,14 +311,13 @@
         carried = nt(v.runs[b], c_b)
         for h in range(NH):
             v.acc[b, hs(h)] = local[hs(h)] * v.e1[b, h : h + 1] + carried[hs(h)] * v.ep[b, h : h + 1]
-        load_z(b).wait()
         zt = v.zv[b].T
         for h in range(NH):
             zz = zt[hs(h)].astype(F32)
             v.sil[b, hs(h)] = zz / (1.0 + jnp.exp(-zz))
         return carry
 
-    lax.fori_loop(0, 2, a2, 0)
+    pairs(0, 2, a2, before=lambda b: load_z(b).wait())
 
     for cp in ex_e:
         cp.wait()
@@ -293,14 +330,14 @@
 
     for j in range(4):
         rows = pl.ds(pl.multiple_of(half + j * HD, HD), HD)
-        v.sz[z, hs(j)] = v.ebuf[0, rows] * hrow(v.dbuf, 1, j) + v.ebuf[1, rows]
+        v.sz[z, hs(j)] = (v.ebuf[0, rows] * hrow(v.dbuf, 1, j) + v.ebuf[1, rows]).astype(BF16)
     ex_z = []
     for d in range(3):
         ex_z.append(remote(v.sz.at[z], v.sz.at[z], v.z_s.at[d, 0], v.z_r.at[d, 0], zpeers[d]))
         ex_z.append(remote(v.dz.at[z], v.dz.at[z], v.z_s.at[d, 1], v.z_r.at[d, 1], zpeers[d]))
     for cp in ex_z:
         cp.start()
-    lax.fori_loop(2, 6, a2, 0)
+    pairs(2, 6, a2, before=lambda b: load_z(b).wait())
 
     for cp in ex_z:
         cp.wait()
@@ -310,11 +347,11 @@
         zpre = zpre + jnp.where(z > k, v.dz[k], 0.0)
     zflip = z + 1 - 2 * lax.rem(z, 2)
     for j in range(4):
-        s01 = v.sz[0, hs(j)] * hrow(v.dz, 1, j) + v.sz[1, hs(j)]
-        s012 = s01 * hrow(v.dz, 2, j) + v.sz[2, hs(j)]
-        v.sy[y, hs(j)] = (s012 * hrow(v.dz, 3, j) + v.sz[3, hs(j)]).astype(BF16)
+        s01 = v.sz[0, hs(j)].astype(F32) * hrow(v.dz, 1, j) + v.sz[1, hs(j)].astype(F32)
+        s012 = s01 * hrow(v.dz, 2, j) + v.sz[2, hs(j)].astype(F32)
+        v.sy[y, hs(j)] = (s012 * hrow(v.dz, 3, j) + v.sz[3, hs(j)].astype(F32)).astype(BF16)
         rows = pl.ds(pl.multiple_of(half + j * HD, HD), HD)
-        v.lev[1, rows] = v.sz[zflip, hs(j)].astype(BF16)
+        v.lev[1, rows] = v.sz[zflip, hs(j)]
         v.lev[2, rows] = s01.astype(BF16)
     ex_y = []
     for d in range(3):
@@ -337,7 +374,7 @@
     set_factor(0, jnp.full((NH, 128), jnp.where(core == 1, 1.0, 0.0), F32))
     set_factor(1, jnp.where(lax.rem(z, 2) == 1, jnp.exp(dpre), 0.0))
     set_factor(2, jnp.where(z >= 2, jnp.exp(dpre + jnp.where(z == 3, v.dz[2], 0.0)), 0.0))
-    lax.fori_loop(6, 8, a2, 0)
+    pairs(6, 8, a2, before=lambda b: load_z(b).wait())
     ld_g.wait()
     for level in (1, 2):
         swap(level).wait()
@@ -357,7 +394,7 @@
             v.acc[b, hs(h)] = v.acc[b, hs(h)] + add
         return carry
 
-    lax.fori_loop(0, 5, b1, 0)
+    pairs(0, 6, b1)
 
     for cp in ex_y:
         cp.wait()
@@ -371,7 +408,7 @@
         swap(level).start()
     set_factor(3, jnp.where(lax.rem(y, 2) == 1, jnp.exp(zpre), 0.0))
     set_factor(4, jnp.where(y >= 2, jnp.exp(zpre + jnp.where(y == 3, v.dy[2], 0.0)), 0.0))
-    lax.fori_loop(5, 8, b1, 0)
+    pairs(6, 8, b1)
     ld_n.wait()
     v.gcol[...] = jnp.broadcast_to(v.ngv[...], (128, CH)).T
     for level in (3, 4):
@@ -392,27 +429,33 @@
             gated = mixed * v.sil[b, hs(h)]
             v.acc[b, hs(h)] = gated
             squares = squares + jnp.sum((gated * gated).reshape(8, 8, BLK), axis=0)
-        v.ssb[head, b] = squares
+        v.ssb[head, b] = jnp.sum(squares, axis=0, keepdims=True)
+        return carry
+
+    def send_q(b):
         for d in range(3):
             ex_q(b, d).start()
-        return carry
-
-    def b3(b, carry):
+
+    def wait_q(b):
         for d in range(3):
             ex_q(b, d).wait()
+
+    def b3(b, carry):
         total = (v.ssb[0, b] + v.ssb[1, b]) + (v.ssb[2, b] + v.ssb[3, b])
-        r = lax.rsqrt(jnp.sum(total, axis=0, keepdims=True) / INNER + 1e-05)
+        r = lax.rsqrt(total / INNER + 1e-05)
         lanes = pl.ds(pl.multiple_of(b * BLK, BLK), BLK)
         for h in range(NH):
             gain = v.gcol[hs(h)]
             n = v.acc[b, hs(h)] * r * jnp.concatenate([gain, gain], axis=1)
             v.nt_[hs(h), lanes] = n.astype(BF16)
-        v.xv[b] = v.nt_[:, lanes].T
-        pltpu.make_async_copy(v.xv.at[b], n_out.at[pl.ds(b * BLK, BLK)], v.s_n.at[b]).start()
         return carry
 
-    lax.fori_loop(0, NB, b2, 0)
-    lax.fori_loop(0, NB, b3, 0)
+    def b4(b, carry):
+        n_out[b] = v.nt_[:, pl.ds(pl.multiple_of(b * BLK, BLK), BLK)].T
+        return carry
+
+    pairs(0, NB, b2, after=send_q)
+    pairs(0, NB, b3, before=wait_q)
 
     ld_cot.wait()
     def ex_p(p):
@@ -446,6 +489,25 @@
                 if m >> 1 == p:
                     ex_r(s, 0, i).start()
 
+    def take(s, t, i):
+        dims = stream_dims(s)
+        m = span(dims[t + 1 :])[i]
+        ex_r(s, t, i).wait()
+        total = v.part[m, hs(s)] + recv_bufs[t][s, i].astype(F32)
+        nxt = sent_masks(s, t + 1)
+        if m in nxt:
+            k = nxt.index(m)
+            v.sb[s, starts[t + 1] + k] = total.astype(BF16)
+            ex_r(s, t + 1, k).start()
+        else:
+            v.part[m, hs(s)] = total
+
+    pending = schedule_events()
+
+    def run_events(now):
+        while pending and pending[0][0] <= now:
+            take(*pending.pop(0)[1:])
+
     for p in range(7, -1, -1):
         sides = []
         for m in (2 * p, 2 * p + 1):
@@ -455,24 +517,13 @@
         v.gsend[p] = nn(v.nt_[pl.ds(other, 256), :], cot).astype(BF16)
         ex_p(p).start()
         v.gown[p] = nn(v.nt_[pl.ds(half, 256), :], cot)
-        if p < 7:
-            finish_pair(p + 1)
-    finish_pair(0)
-
-    for t in range(3):
-        for s in range(4):
-            dims = stream_dims(s)
-            kept = span(dims[t + 1 :])
-            nxt = sent_masks(s, t + 1)
-            for i, m in enumerate(kept):
-                ex_r(s, t, i).wait()
-                total = v.part[m, hs(s)] + recv_bufs[t][s, i].astype(F32)
-                if m in nxt:
-                    k = nxt.index(m)
-                    v.sb[s, starts[t + 1] + k] = total.astype(BF16)
-                    ex_r(s, t + 1, k).start()
-                else:
-                    v.part[m, hs(s)] = total
+        if p + LAG < 8:
+            finish_pair(p + LAG)
+            run_events(7 - p)
+    for p in range(LAG - 1, -1, -1):
+        finish_pair(p)
+        run_events(7 - p + LAG)
+    run_events(1000)
     for s in range(4):
         ex_r(s, 3, 0).wait()
         v.gt[:, hs(s)] = (v.part[0, hs(s)] + v.r3[s, 0].astype(F32)).T
@@ -514,57 +565,62 @@
             ex_a(s, t, 0).start()
     for s in range(4):
         ex_c(s, 0).start()
-    for t in range(4):
-        for i in range(1 << t):
-            for s in range(4):
-                ex_a(s, t, i).wait_recv()
-                got = (1 << t) + i
-                for later in range(t + 1, 4):
-                    ex_a(s, later, got).start()
-                ex_c(s, got).start()
+    lax.fori_loop(0, NB, b4, 0)
+    for got in sorted(range(1, 16), key=lambda k: (bin(k).count("1"), k)):
+        t = got.bit_length() - 1
+        for s in range(4):
+            ex_a(s, t, got - (1 << t)).wait_recv()
+            for later in range(t + 1, 4):
+                ex_a(s, later, got).start()
+            ex_c(s, got).start()
     ex_g.wait()
-    mine = pl.ds(pl.multiple_of(core * 64, 64), 64)
-    outs = [
-        pltpu.make_async_copy(v.gt.at[mine], g_out.at[:, pl.ds(half, 256)], v.s_out.at[0]),
-        pltpu.make_async_copy(v.gx, g_out.at[:, pl.ds(other, 256)], v.s_out.at[1]),
-        pltpu.make_async_copy(v.w.at[:, core], w_out.at[:, :, pl.ds(half, 256)], v.s_out.at[2]),
-    ]
-    for cp in outs:
-        cp.start()
+    gt_out[...] = v.gt[pl.ds(pl.multiple_of(core * 64, 64), 64)]
     for s in range(4):
         for i in range(16):
             ex_c(s, i).wait()
-    last = pltpu.make_async_copy(v.w.at[:, 1 - core], w_out.at[:, :, pl.ds(other, 256)], v.s_out.at[3])
-    last.start()
     for s in range(4):
         for t in range(4):
             for i in range(1 << t):
                 ex_a(s, t, i).wait_send()
-    for b in range(NB):
-        pltpu.make_async_copy(v.xv.at[b], n_out.at[pl.ds(b * BLK, BLK)], v.s_n.at[b]).wait()
-    for cp in outs:
+
+
+def writer(n_v, w_v, gt_v, gx_v, n_out, w_out, g_out, sems):
+    core = lax.rem(lax.axis_index("ctx"), 2)
+    half = pl.multiple_of(core * 256, 256)
+    other = pl.multiple_of((1 - core) * 256, 256)
+    copies = [
+        pltpu.make_async_copy(w_v.at[:, 0], w_out.at[:, :, pl.ds(0, 256)], sems.at[0]),
+        pltpu.make_async_copy(w_v.at[:, 1], w_out.at[:, :, pl.ds(256, 256)], sems.at[1]),
+        pltpu.make_async_copy(n_v, n_out, sems.at[2]),
+        pltpu.make_async_copy(gt_v, g_out.at[:, pl.ds(half, 256)], sems.at[3]),
+        pltpu.make_async_copy(gx_v, g_out.at[:, pl.ds(other, 256)], sems.at[4]),
+    ]
+    for cp in copies:
+        cp.start()
+    for cp in copies:
         cp.wait()
-    last.wait()
 
 
 def on_device(
     entries, gating, state_in, state_out, step_size, decay_rate, skip_gain, level_gate,
     norm_gain, cotangent, master_weight, first_moment, second_moment,
 ):
-    anyspace = pl.BlockSpec(memory_space=pl.ANY)
+    hbm = pl.BlockSpec(memory_space=pltpu.HBM)
     smem = pl.BlockSpec(memory_space=pltpu.SMEM)
-    normed, weights, gradient = pl.pallas_call(
+    vmem = pl.BlockSpec(memory_space=pltpu.VMEM)
+    parts = pl.pallas_call(
         kernel,
         out_shape=(
-            jax.ShapeDtypeStruct((NB * BLK, CH), BF16),
-            jax.ShapeDtypeStruct((16, 128, CH), BF16),
-            jax.ShapeDtypeStruct((64, CH), F32),
+            pltpu.VMEM((NB, BLK, CH), BF16),
+            pltpu.VMEM((16, 2, 128, 256), BF16),
+            pltpu.VMEM((64, 256), F32),
+            pltpu.VMEM((64, 256), F32),
         ),
-        in_specs=[anyspace] * 5 + [smem] * 2 + [anyspace] * 6,
-        out_specs=(anyspace,) * 3,
+        in_specs=[hbm] * 5 + [smem] * 2 + [hbm] * 6,
+        out_specs=(vmem,) * 4,
         scratch_shapes=list(SCRATCH.values()),
         compiler_params=pltpu.CompilerParams(
-            collective_id=0, has_side_effects=True, vmem_limit_bytes=60 * 1024 * 1024
+            collective_id=0, has_side_effects=True, vmem_limit_bytes=59 * 1024 * 1024
         ),
     )(
         entries,
@@ -581,7 +637,19 @@
         first_moment,
         second_moment,
     )
-    return normed, weights.reshape(DM, CH), gradient
+    normed, weights, gradient = pl.pallas_call(
+        writer,
+        out_shape=(
+            jax.ShapeDtypeStruct((NB, BLK, CH), BF16),
+            jax.ShapeDtypeStruct((16, 128, CH), BF16),
+            jax.ShapeDtypeStruct((64, CH), F32),
+        ),
+        in_specs=[vmem] * 4,
+        out_specs=(hbm,) * 3,
+        scratch_shapes=[pltpu.SemaphoreType.DMA((5,))],
+        compiler_params=pltpu.CompilerParams(vmem_limit_bytes=1024 * 1024),
+    )(*parts)
+    return normed.reshape(NB * BLK, CH), weights.reshape(DM, CH), gradient
 
 
 def solution(mesh):

time: 86.8 us -> 69 us (0.79)
  Pallas kernels: 80.9 us -> 68.3 us
  local copies, waits for them, and re-layouts: 5.18 us -> 0 us
    pallas_call x1 -> x2, Pallas kernels: 80.9 us -> 68.3 us  [the longest x1 66.2 us: on_device(): pl.pallas_call(kernel, out_shape=(pltpu.VMEM((NB, BLK, CH), BF16), pltpu....]
    unnamed x7 -> x0, local copies, waits for them, and re-layouts: 5.18 us -> none
where the time goes in v2:
time: 69 us; the launch traced here: 68.9 us
  Pallas kernels  68.3 us (99%)
    pallas_call x1, Pallas kernels, on_device(): pl.pallas_call(kernel, out_shape=(pltpu.VMEM((NB, BLK, CH), BF16), pltpu....  66.2 us
    pallas_call x1, Pallas kernels, on_device(): pl.pallas_call(writer, out_shape=(jax.ShapeDtypeStruct((NB, BLK, CH), BF1...  2.08 us

profile of v2, /device:TPU:1, one launch (start us, length us, event | category | flops | bytes accessed | tf_op | source)
XLA Modules:
  0.0 68.9 jit_solution(8266625806187535730)
XLA Ops:
  0.6 66.2 %shard_map.148 = (bf16[8,256,512]{2,1,0:T(8,128)(2,1)S(1)}, bf16[16,2,128,256]{3,2,1,0:T(8,128)(2,1)S(1)}, f32[64,256]{1,0:T(8,128)S(1)}, f32[64,256]{1,0:T(8,128)S(1)}) custom-call(bf16[2048,512]{1,0:T(8,128)(2,1)} %x_h.1, bf16[2048,512]{1,0:T(8,128)(2,1)} %z_h.1, bf16[8,256,128]{2,1,0:T(8,128)(2,1)} %bitcast.6, bf16[8,256,128]{2,1,0:T(8,128)(2,1)} %bitcast.7, ...), custom_call_target="tpu_custom_call" | custom-call | tf_op jit(solution)/shard_map/pallas_call | solution.py:611
  66.8 2.1 %shard_map.149 = (bf16[8,256,512]{2,1,0:T(8,128)(2,1)}, bf16[16,128,512]{2,1,0:T(8,128)(2,1)}, f32[64,512]{1,0:T(8,128)}) custom-call(bf16[8,256,512]{2,1,0:T(8,128)(2,1)S(1)} %get-tuple-element.10.n_v, bf16[16,2,128,256]{3,2,1,0:T(8,128)(2,1)S(1)} %get-tuple-element.11.w_v, f32[64,256]{1,0:T(8,128)S(1)} %get-tuple-element.12.gt_v, ...), custom_call_target="tpu_custom_call" | custom-call | tf_op jit(solution)/shard_map/pallas_call | solution.py:640

commit v3 on v2

--- a/solution.py
+++ b/solution.py
@@ -41,7 +41,7 @@
 
 
 def stream_dims(s):
-    return [(s + t) % DIMS for t in range(DIMS)]
+    return [((0, 2, 1, 3)[s] + t) % DIMS for t in range(DIMS)]
 
 
 def span(dims):
@@ -51,27 +51,37 @@
     return masks
 
 
-LAG = 2
-HOP = 3
-
-
-def schedule_events():
+LAG = 4
+HOP = 6
+UPDATE = 2
+
+
+def group_of(s):
+    return s // 2
+
+
+def schedule():
     out = []
+    ready = [0, 0]
     for s in range(4):
         dims = stream_dims(s)
-        sent = {}
-        done = {m: 7 - (m >> 1) + LAG for m in range(16)}
-        for m in range(16):
-            if m >> dims[0] & 1:
-                sent[m] = done[m]
-        for t in range(3):
+        done = {m: 8 * group_of(s) + 7 - (m >> 1) + LAG for m in range(16)}
+        sent = {m: done[m] for m in range(16) if m >> dims[0] & 1}
+        for t in range(4):
             for i, m in enumerate(span(dims[t + 1 :])):
                 when = max(sent[m | 1 << dims[t]] + HOP, done[m])
                 done[m] = when
-                out.append((when, s, t, i))
-                if m >> dims[t + 1] & 1:
+                out.append((when, 0, t, i, s))
+                if t < 3 and m >> dims[t + 1] & 1:
                     sent[m] = when
-    return sorted(out, key=lambda e: (e[0], e[2], e[3], e[1]))
+        ready[group_of(s)] = max(ready[group_of(s)], done[0])
+    for g in range(2):
+        out.append((ready[g], 1, g))
+        for got in range(1, 16):
+            hops = bin(got).count("1")
+            for s in (2 * g, 2 * g + 1):
+                out.append((ready[g] + UPDATE + HOP * hops, 2, got, s))
+    return sorted(out)
 
 
 SCRATCH = dict(
@@ -93,7 +103,7 @@
     ep=pltpu.VMEM((NB, NH, BLK), F32),
     e1=pltpu.VMEM((NB, NH, BLK), F32),
     ecum=pltpu.VMEM((NB, NH, BLK), F32),
-    ebuf=pltpu.VMEM((2, CH, ST), F32),
+    ebuf=pltpu.VMEM((2, CH, ST), BF16),
     dbuf=pltpu.VMEM((2, NH, 128), F32),
     sz=pltpu.VMEM((4, CH // 2, ST), BF16),
     dz=pltpu.VMEM((4, NH, 128), F32),
@@ -104,9 +114,9 @@
     ssb=pltpu.VMEM((4, NB, 1, BLK), F32),
     nt_=pltpu.VMEM((CH, NB * BLK), BF16),
     cotv=pltpu.VMEM((NB * BLK, DM), BF16),
-    gsend=pltpu.VMEM((8, 256, 256), BF16),
-    gown=pltpu.VMEM((8, 256, 256), F32),
-    grecv=pltpu.VMEM((8, 256, 256), BF16),
+    gsend=pltpu.VMEM((2, 8, 128, 256), BF16),
+    gown=pltpu.VMEM((2, 8, 128, 256), F32),
+    grecv=pltpu.VMEM((2, 8, 128, 256), BF16),
     part=pltpu.VMEM((16, 256, 128), F32),
     sb=pltpu.VMEM((4, 15, HD, 128), BF16),
     r0=pltpu.VMEM((4, 8, HD, 128), BF16),
@@ -119,8 +129,8 @@
     s_z=pltpu.SemaphoreType.DMA((NB,)),
     s_in=pltpu.SemaphoreType.DMA((6,)),
     s_m=pltpu.SemaphoreType.DMA((3,)),
-    e_s=pltpu.SemaphoreType.DMA((2,)),
-    e_r=pltpu.SemaphoreType.DMA((2,)),
+    e_s=pltpu.SemaphoreType.DMA((3,)),
+    e_r=pltpu.SemaphoreType.DMA((3,)),
     z_s=pltpu.SemaphoreType.DMA((3, 2)),
     z_r=pltpu.SemaphoreType.DMA((3, 2)),
     y_s=pltpu.SemaphoreType.DMA((3, 2)),
@@ -131,8 +141,8 @@
     q_r=pltpu.SemaphoreType.DMA((NB, 3)),
     m_s=pltpu.SemaphoreType.DMA((3,)),
     m_r=pltpu.SemaphoreType.DMA((3,)),
-    p_s=pltpu.SemaphoreType.DMA((8,)),
-    p_r=pltpu.SemaphoreType.DMA((8,)),
+    p_s=pltpu.SemaphoreType.DMA((2, 8)),
+    p_r=pltpu.SemaphoreType.DMA((2, 8)),
     r_s=pltpu.SemaphoreType.DMA((4, 15)),
     r_r=pltpu.SemaphoreType.DMA((4, 15)),
     g_s=pltpu.SemaphoreType.DMA((1,)),
@@ -288,13 +298,15 @@
 
     ld_b.wait()
     dsum = pairs(0, NB, a1, before=lambda b: load_x(b).wait(), carry=jnp.zeros((NH, BLK), F32))
-    v.ebuf[core] = v.run[...]
+    v.ebuf[core] = v.run[...].astype(BF16)
     v.dbuf[core] = dsum[:, :128]
 
     pl.semaphore_wait(barrier, 10)
+    first, rest = v.ebuf.at[core, pl.ds(other, 256)], v.ebuf.at[core, pl.ds(half, 256)]
     ex_e = [
-        remote(v.ebuf.at[core], v.ebuf.at[core], v.e_s.at[0], v.e_r.at[0], partner),
         remote(v.dbuf.at[core], v.dbuf.at[core], v.e_s.at[1], v.e_r.at[1], partner),
+        remote(first, first, v.e_s.at[0], v.e_r.at[0], partner),
+        remote(rest, rest, v.e_s.at[2], v.e_r.at[2], partner),
     ]
     for cp in ex_e:
         cp.start()
@@ -319,7 +331,7 @@
 
     pairs(0, 2, a2, before=lambda b: load_z(b).wait())
 
-    for cp in ex_e:
+    for cp in ex_e[:2]:
         cp.wait()
     d0, d1 = v.dbuf[0], v.dbuf[1]
     v.dz[z] = d0 + d1
@@ -330,7 +342,9 @@
 
     for j in range(4):
         rows = pl.ds(pl.multiple_of(half + j * HD, HD), HD)
-        v.sz[z, hs(j)] = (v.ebuf[0, rows] * hrow(v.dbuf, 1, j) + v.ebuf[1, rows]).astype(BF16)
+        v.sz[z, hs(j)] = (
+            v.ebuf[0, rows].astype(F32) * hrow(v.dbuf, 1, j) + v.ebuf[1, rows].astype(F32)
+        ).astype(BF16)
     ex_z = []
     for d in range(3):
         ex_z.append(remote(v.sz.at[z], v.sz.at[z], v.z_s.at[d, 0], v.z_r.at[d, 0], zpeers[d]))
@@ -366,7 +380,8 @@
 
     for level in (1, 2):
         swap(level).start()
-    v.lev[0] = v.ebuf[0].astype(BF16)
+    ex_e[2].wait()
+    v.lev[0] = v.ebuf[0]
 
     def set_factor(level, value):
         v.fac[level] = jnp.concatenate([value, value], axis=1)
@@ -458,8 +473,8 @@
     pairs(0, NB, b3, before=wait_q)
 
     ld_cot.wait()
-    def ex_p(p):
-        return remote(v.gsend.at[p], v.grecv.at[p], v.p_s.at[p], v.p_r.at[p], partner)
+    def ex_p(g, p):
+        return remote(v.gsend.at[g, p], v.grecv.at[g, p], v.p_s.at[g, p], v.p_r.at[g, p], partner)
 
     recv_bufs = (v.r0, v.r1, v.r2, v.r3)
     starts = (0, 8, 12, 14)
@@ -473,28 +488,30 @@
         k = starts[t] + i
         return remote(v.sb.at[s, k], recv_bufs[t].at[s, i], v.r_s.at[s, k], v.r_r.at[s, k], cube[dims[t]])
 
-    def finish_pair(p):
-        ex_p(p).wait()
+    def finish_pair(g, p):
+        ex_p(g, p).wait()
+        streams = (2 * g, 2 * g + 1)
         for a in range(2):
             lanes = slice(a * 128, (a + 1) * 128)
             m = 2 * p + a
-            total = v.gown[p, :, lanes] + v.grecv[p, :, lanes].astype(F32)
-            for s in range(4):
-                if m >> s & 1:
-                    v.sb[s, sent_masks(s, 0).index(m)] = total[hs(s)].astype(BF16)
+            total = v.gown[g, p, :, lanes] + v.grecv[g, p, :, lanes].astype(F32)
+            for s in streams:
+                rows = total[hs(s % 2)]
+                if m >> stream_dims(s)[0] & 1:
+                    v.sb[s, sent_masks(s, 0).index(m)] = rows.astype(BF16)
                 else:
-                    v.part[m, hs(s)] = total[hs(s)]
-        for s in range(4):
+                    v.part[m, hs(s)] = rows
+        for s in streams:
             for i, m in enumerate(sent_masks(s, 0)):
                 if m >> 1 == p:
                     ex_r(s, 0, i).start()
 
-    def take(s, t, i):
+    def take(t, i, s):
         dims = stream_dims(s)
         m = span(dims[t + 1 :])[i]
         ex_r(s, t, i).wait()
         total = v.part[m, hs(s)] + recv_bufs[t][s, i].astype(F32)
-        nxt = sent_masks(s, t + 1)
+        nxt = sent_masks(s, t + 1) if t < 3 else []
         if m in nxt:
             k = nxt.index(m)
             v.sb[s, starts[t + 1] + k] = total.astype(BF16)
@@ -502,79 +519,82 @@
         else:
             v.part[m, hs(s)] = total
 
-    pending = schedule_events()
+    own = y * 4 + z
+
+    def update(g):
+        cols = slice(g * 128, (g + 1) * 128)
+        grad = v.part[0, cols].T
+        v.gt[:, cols] = grad
+        one = 0.9 * v.mw[1, :, cols] + 0.1 * grad
+        two = 0.95 * v.mw[2, :, cols] + 0.05 * grad * grad
+        ratio = one / (1.0 - 0.9**10) / (jnp.sqrt(two / (1.0 - 0.95**10)) + 1e-08)
+        master = v.mw[0, :, cols]
+        v.w[own, core, g] = (master - 0.1 * (ratio + 0.1 * master)).astype(BF16)
+        for t in range(4):
+            for s in (2 * g, 2 * g + 1):
+                ex_a(s, t, 0).start()
+        for s in (2 * g, 2 * g + 1):
+            ex_c(s, 0).start()
+
+    def slot(m):
+        yy, zz = flip(y, z, m)
+        return yy * 4 + zz
+
+    def piece_of(s, m):
+        return v.w.at[slot(m), core, group_of(s), pl.ds(s % 2 * 64, 64)]
+
+    def ex_a(s, t, i):
+        dims = stream_dims(s)
+        piece = piece_of(s, span(dims[:t])[i])
+        k = (1 << t) - 1 + i
+        return remote(piece, piece, v.a_s.at[s, k], v.a_r.at[s, k], cube[dims[t]])
+
+    def ex_c(s, i):
+        piece = piece_of(s, span(stream_dims(s))[i])
+        return remote(piece, piece, v.c_s.at[s, i], v.c_r.at[s, i], partner)
+
+    def forward(got, s):
+        t = got.bit_length() - 1
+        ex_a(s, t, got - (1 << t)).wait_recv()
+        for later in range(t + 1, 4):
+            ex_a(s, later, got).start()
+        ex_c(s, got).start()
+
+    pending = schedule()
 
     def run_events(now):
         while pending and pending[0][0] <= now:
-            take(*pending.pop(0)[1:])
-
-    for p in range(7, -1, -1):
-        sides = []
-        for m in (2 * p, 2 * p + 1):
-            yy, zz = flip(y, z, m)
-            sides.append(v.cotv[:, pl.ds(pl.multiple_of((yy * 4 + zz) * 128, 128), 128)])
-        cot = jnp.concatenate(sides, axis=1)
-        v.gsend[p] = nn(v.nt_[pl.ds(other, 256), :], cot).astype(BF16)
-        ex_p(p).start()
-        v.gown[p] = nn(v.nt_[pl.ds(half, 256), :], cot)
-        if p + LAG < 8:
-            finish_pair(p + LAG)
-            run_events(7 - p)
-    for p in range(LAG - 1, -1, -1):
-        finish_pair(p)
-        run_events(7 - p + LAG)
-    run_events(1000)
-    for s in range(4):
-        ex_r(s, 3, 0).wait()
-        v.gt[:, hs(s)] = (v.part[0, hs(s)] + v.r3[s, 0].astype(F32)).T
+            (take, update, forward)[pending[0][1]](*pending.pop(0)[2:])
+
+    for cp in ld_m:
+        cp.wait()
+    for cp in ex_m:
+        cp.wait()
+    products = [(g, p) for g in range(2) for p in range(7, -1, -1)]
+    for step in range(len(products) + LAG):
+        if step < len(products):
+            g, p = products[step]
+            sides = []
+            for m in (2 * p, 2 * p + 1):
+                yy, zz = flip(y, z, m)
+                sides.append(v.cotv[:, pl.ds(pl.multiple_of((yy * 4 + zz) * 128, 128), 128)])
+            rows = [v.nt_[pl.ds(pl.multiple_of(side + g * 128, 128), 128), :] for side in (other, half)]
+            product = nn(jnp.concatenate(rows, axis=0), jnp.concatenate(sides, axis=1))
+            v.gsend[g, p] = product[:128].astype(BF16)
+            ex_p(g, p).start()
+            v.gown[g, p] = product[128:]
+        if step >= LAG:
+            finish_pair(*products[step - LAG])
+            run_events(step)
+    lax.fori_loop(0, NB, b4, 0)
+    run_events(10000)
 
     ex_g = remote(
         v.gt.at[pl.ds(pl.multiple_of((1 - core) * 64, 64), 64)], v.gx, v.g_s.at[0], v.g_r.at[0], partner
     )
     ex_g.start()
-    for cp in ld_m:
-        cp.wait()
-    for cp in ex_m:
-        cp.wait()
-    own = y * 4 + z
-    grad = v.gt[...]
-    one = 0.9 * v.mw[1] + 0.1 * grad
-    two = 0.95 * v.mw[2] + 0.05 * grad * grad
-    ratio = one / (1.0 - 0.9**10) / (jnp.sqrt(two / (1.0 - 0.95**10)) + 1e-08)
-    master = v.mw[0]
-    v.w[own, core] = (master - 0.1 * (ratio + 0.1 * master)).astype(BF16)
-
-    def slot(m):
-        yy, zz = flip(y, z, m)
-        return yy * 4 + zz
-
-    def ex_a(s, t, i):
-        dims = stream_dims(s)
-        m = span(dims[:t])[i]
-        piece = v.w.at[slot(m), core, pl.ds(s * 32, 32)]
-        k = (1 << t) - 1 + i
-        return remote(piece, piece, v.a_s.at[s, k], v.a_r.at[s, k], cube[dims[t]])
-
-    def ex_c(s, i):
-        m = span(stream_dims(s))[i]
-        piece = v.w.at[slot(m), core, pl.ds(s * 32, 32)]
-        return remote(piece, piece, v.c_s.at[s, i], v.c_r.at[s, i], partner)
-
-    for t in range(4):
-        for s in range(4):
-            ex_a(s, t, 0).start()
-    for s in range(4):
-        ex_c(s, 0).start()
-    lax.fori_loop(0, NB, b4, 0)
-    for got in sorted(range(1, 16), key=lambda k: (bin(k).count("1"), k)):
-        t = got.bit_length() - 1
-        for s in range(4):
-            ex_a(s, t, got - (1 << t)).wait_recv()
-            for later in range(t + 1, 4):
-                ex_a(s, later, got).start()
-            ex_c(s, got).start()
+    gt_out[...] = v.gt[pl.ds(pl.multiple_of(core * 64, 64), 64)]
     ex_g.wait()
-    gt_out[...] = v.gt[pl.ds(pl.multiple_of(core * 64, 64), 64)]
     for s in range(4):
         for i in range(16):
             ex_c(s, i).wait()
@@ -589,11 +609,15 @@
     half = pl.multiple_of(core * 256, 256)
     other = pl.multiple_of((1 - core) * 256, 256)
     copies = [
-        pltpu.make_async_copy(w_v.at[:, 0], w_out.at[:, :, pl.ds(0, 256)], sems.at[0]),
-        pltpu.make_async_copy(w_v.at[:, 1], w_out.at[:, :, pl.ds(256, 256)], sems.at[1]),
-        pltpu.make_async_copy(n_v, n_out, sems.at[2]),
-        pltpu.make_async_copy(gt_v, g_out.at[:, pl.ds(half, 256)], sems.at[3]),
-        pltpu.make_async_copy(gx_v, g_out.at[:, pl.ds(other, 256)], sems.at[4]),
+        pltpu.make_async_copy(w_v.at[:, k // 2, k % 2], w_out.at[:, :, pl.ds(k * 128, 128)], sems.at[k])
+        for k in range(4)
+    ]
+    copies += [
+        pltpu.make_async_copy(n_v.at[pl.ds(k * 2, 2)], n_out.at[pl.ds(k * 2, 2)], sems.at[4 + k]) for k in range(4)
+    ]
+    copies += [
+        pltpu.make_async_copy(gt_v, g_out.at[:, pl.ds(half, 256)], sems.at[8]),
+        pltpu.make_async_copy(gx_v, g_out.at[:, pl.ds(other, 256)], sems.at[9]),
     ]
     for cp in copies:
         cp.start()
@@ -612,7 +636,7 @@
         kernel,
         out_shape=(
             pltpu.VMEM((NB, BLK, CH), BF16),
-            pltpu.VMEM((16, 2, 128, 256), BF16),
+            pltpu.VMEM((16, 2, 2, 128, 128), BF16),
             pltpu.VMEM((64, 256), F32),
             pltpu.VMEM((64, 256), F32),
         ),
@@ -646,7 +670,7 @@
         ),
         in_specs=[vmem] * 4,
         out_specs=(hbm,) * 3,
-        scratch_shapes=[pltpu.SemaphoreType.DMA((5,))],
+        scratch_shapes=[pltpu.SemaphoreType.DMA((10,))],
         compiler_params=pltpu.CompilerParams(vmem_limit_bytes=1024 * 1024),
     )(*parts)
     return normed.reshape(NB * BLK, CH), weights.reshape(DM, CH), gradient

time: 69 us -> 74.3 us (1.077)
  Pallas kernels: 68.3 us -> 73.3 us
    pallas_call x1, Pallas kernels: 66.2 us -> 71.2 us  [on_device(): pl.pallas_call(kernel, out_shape=(pltpu.VMEM((NB, BLK, CH), BF16), pltpu....]
where the time goes in v3:
time: 74.3 us; the launch traced here: 74.1 us
  Pallas kernels  73.3 us (99%)
  between operations  0.8 us (1%)
    pallas_call x1, Pallas kernels, on_device(): pl.pallas_call(kernel, out_shape=(pltpu.VMEM((NB, BLK, CH), BF16), pltpu....  71.2 us
    pallas_call x1, Pallas kernels, on_device(): pl.pallas_call(writer, out_shape=(jax.ShapeDtypeStruct((NB, BLK, CH), BF1...  2.12 us

profile of v3, /device:TPU:1, one launch (start us, length us, event | category | flops | bytes accessed | tf_op | source)
XLA Modules:
  0.0 74.1 jit_solution(865042176861016374)
XLA Ops:
  0.6 71.2 %shard_map.148 = (bf16[8,256,512]{2,1,0:T(8,128)(2,1)S(1)}, bf16[16,2,2,128,128]{4,3,2,1,0:T(8,128)(2,1)S(1)}, f32[64,256]{1,0:T(8,128)S(1)}, f32[64,256]{1,0:T(8,128)S(1)}) custom-call(bf16[2048,512]{1,0:T(8,128)(2,1)} %x_h.1, bf16[2048,512]{1,0:T(8,128)(2,1)} %z_h.1, bf16[8,256,128]{2,1,0:T(8,128)(2,1)} %bitcast.6, bf16[8,256,128]{2,1,0:T(8,128)(2,1)} %bitcast.7, ...), custom_call_target="tpu_custom_call" | custom-call | tf_op jit(solution)/shard_map/pallas_call | solution.py:635
  71.9 2.1 %shard_map.149 = (bf16[8,256,512]{2,1,0:T(8,128)(2,1)}, bf16[16,128,512]{2,1,0:T(8,128)(2,1)}, f32[64,512]{1,0:T(8,128)}) custom-call(bf16[8,256,512]{2,1,0:T(8,128)(2,1)S(1)} %get-tuple-element.10.n_v, bf16[16,2,2,128,128]{4,3,2,1,0:T(8,128)(2,1)S(1)} %get-tuple-element.11.w_v, f32[64,256]{1,0:T(8,128)S(1)} %get-tuple-element.12.gt_v, ...), custom_call_target="tpu_custom_call" | custom-call | tf_op jit(solution)/shard_map/pallas_call | solution.py:664
